TPU v7x, 32 devices: a whole 2x2x4 slice. The times are simulated.
32 devices in a mesh: dp: 8 (over y, x, core), fsdp: 4 (over z).
Axes of the slice: x: 2, y: 2, z: 4, core: 2. Of those that a mesh axis runs over, the one named last changes fastest.
Arguments:
- inputs: bfloat16 [12288, 1024], P(('dp', 'fsdp')), may hold values from -6 to 6
- cotangent: bfloat16 [12288, 1024], P(('dp', 'fsdp')), may hold values from -6 to 6
- lengths: int32 [64, 3], P(('dp', 'fsdp')), may hold values from 0 to 192, as said below
- buckets: int32 [64], P(('dp', 'fsdp')), may hold values from 0 to 2, as said below
- ffn1_in: bfloat16 [1024, 4096], P('fsdp'), may hold values from -0.1875 to 0.1875
- ffn1_out: bfloat16 [4096, 1024], P('fsdp'), may hold values from -0.09375 to 0.09375
- attn_in: bfloat16 [1024, 4096], P('fsdp'), may hold values from -0.1875 to 0.1875
- attn_out: bfloat16 [1024, 1024], P('fsdp'), may hold values from -0.5 to 0.5
- conv_in: bfloat16 [1024, 2048], P('fsdp'), may hold values from -0.1875 to 0.1875
- conv_out: bfloat16 [1024, 1024], P('fsdp'), may hold values from -0.1875 to 0.1875
- ffn2_in: bfloat16 [1024, 4096], P('fsdp'), may hold values from -0.1875 to 0.1875
- ffn2_out: bfloat16 [4096, 1024], P('fsdp'), may hold values from -0.09375 to 0.09375
- norm_gains: bfloat16 [6, 1024], P(None, 'fsdp'), may hold values from 0.5 to 1.5
- pos_bias: bfloat16 [2, 1024], P(None, 'fsdp'), may hold values from -6 to 6
- kernel: bfloat16 [5, 1024], P(None, 'fsdp'), may hold values from -2.5 to 2.5
Outputs:
- outputs: bfloat16 [12288, 1024], P(('dp', 'fsdp'))
- grad_inputs: float32 [12288, 1024], P(('dp', 'fsdp'))
- grad_ffn1_in: float32 [1024, 4096], P('fsdp')
- grad_ffn1_out: float32 [4096, 1024], P('fsdp')
- grad_attn_in: float32 [1024, 4096], P('fsdp')
- grad_attn_out: float32 [1024, 1024], P('fsdp')
- grad_conv_in: float32 [1024, 2048], P('fsdp')
- grad_conv_out: float32 [1024, 1024], P('fsdp')
- grad_ffn2_in: float32 [1024, 4096], P('fsdp')
- grad_ffn2_out: float32 [4096, 1024], P('fsdp')
- grad_norm_gains: float32 [6, 1024], P(None, 'fsdp')
- grad_pos_bias: float32 [2, 1024], P(None, 'fsdp')
- grad_kernel: float32 [5, 1024], P(None, 'fsdp')
Inputs may be any that keep to these rules, and one draw needn't show every extreme that they name: `buckets`: bucket id of each micro-batch; its bucket holds 64 * (id + 1) frames; micro-batch 0 has id 2. lengths[m, s] is the frame count of slot s of micro-batch m: slot s holds an utterance when s < 192 // (64 * (id + 1)), of a quarter of the bucket to the whole bucket, slot 0 exactly the whole bucket; other slots hold 0.
All inputs are finite; a program needn't handle non-finite values.
Results may differ from a plain program's by a relative error of at most 0.023.
Values may be sent and summed in bfloat16 or wider, within the bound.
A program may use at most 256 MiB of HBM per device.

v0:
```python
from functools import partial
import math

import jax
import jax.numpy as jnp
from jax import lax
from jax.experimental import pallas as pl
from jax.experimental.pallas import tpu as pltpu
from jax.sharding import PartitionSpec as P

MESH = pl.DeviceIdType.MESH

D = 1024
HEADS = 8
HEAD_DIM = 128
KERNEL = 5
BUCKET = 64
MICRO = 2
FRAMES = 192
SLOTS = 3


def matmul(left_side, right_side):
    return jnp.dot(left_side, right_side, preferred_element_type=jnp.float32)


def left_product(left_side, right_side):
    return lax.dot_general(
        left_side, right_side, (((0,), (0,)), ((), ())), preferred_element_type=jnp.float32
    )


def right_product(left_side, right_side):
    return lax.dot_general(
        left_side, right_side, (((1,), (1,)), ((), ())), preferred_element_type=jnp.float32
    )


def layer_norm(values, gain_row):
    centred = values - jnp.mean(values, axis=-1, keepdims=True)
    spread = jnp.mean(centred * centred, axis=-1, keepdims=True)
    return centred * lax.rsqrt(spread + 1e-05) * gain_row


def swish_act(values):
    return values * jax.nn.sigmoid(values)


def neighbour(values, offset):
    if offset > 0:
        filler = jnp.zeros((offset,) + values.shape[1:], values.dtype)
        return jnp.concatenate([values[offset:], filler], axis=0)
    if offset < 0:
        filler = jnp.zeros((-offset,) + values.shape[1:], values.dtype)
        return jnp.concatenate([filler, values[:offset]], axis=0)
    return values


def frame_plan(utter_len, bucket_id):
    position = jnp.arange(FRAMES, dtype=jnp.int32)
    bucket_len = BUCKET * (bucket_id + 1)
    segment = position // bucket_len
    offset_in = position - segment * bucket_len
    slot_index = jnp.arange(SLOTS, dtype=jnp.int32)
    slot_limit = jnp.sum(
        jnp.where(segment[:, None] == slot_index[None, :], utter_len[None, :], 0), axis=1
    )
    is_valid = offset_in < slot_limit
    allowed = (segment[:, None] == segment[None, :]) & is_valid[None, :] | (
        position[:, None] == position[None, :]
    )
    tap_list = []
    for tap_index in range(KERNEL):
        shift_by = tap_index - KERNEL // 2
        same_slot = (neighbour(segment + 1, shift_by) == segment + 1) & neighbour(
            is_valid, shift_by
        )
        tap_list.append(same_slot.astype(jnp.float32))
    return (allowed, jnp.stack(tap_list, axis=0))


def sinusoid(sign):
    column = jnp.arange(D, dtype=jnp.int32)
    rates = jnp.exp((column // 2).astype(jnp.float32) * (-2.0 * math.log(10000.0) / D))
    phase = (column % 2).astype(jnp.float32) * (0.5 * math.pi)
    coarse = sign * (16 * jnp.arange(2 * FRAMES // 16, dtype=jnp.int32) - (FRAMES - 1)).astype(jnp.float32)
    fine = sign * jnp.arange(16, dtype=jnp.int32).astype(jnp.float32)
    angle = coarse[:, None] * rates[None, :]
    rest = fine[:, None] * rates[None, :] + phase[None, :]
    sin_a, cos_a = lax.optimization_barrier((jnp.sin(angle), jnp.cos(angle)))
    sin_b, cos_b = lax.optimization_barrier((jnp.sin(rest), jnp.cos(rest)))
    table = sin_a[:, None] * cos_b[None] + cos_a[:, None] * sin_b[None]
    return table.reshape(2 * FRAMES, D)


def depthwise(values, kernel_rows, tap_masks):
    running = jnp.zeros_like(values)
    for tap_index in range(KERNEL):
        moved = neighbour(values, tap_index - KERNEL // 2)
        running = running + moved * tap_masks[tap_index][:, None] * kernel_rows[tap_index][None, :]
    return running


def conv_inner(gated, gain_inner, kernel_rows, tap_masks):
    gated_out = gated[:, :D] * jax.nn.sigmoid(gated[:, D:])
    return swish_act(layer_norm(depthwise(gated_out, kernel_rows, tap_masks), gain_inner))


def ffn_forward(values, gain_row, weight_in, weight_out):
    normed, norm_pull = jax.vjp(layer_norm, values, gain_row)
    normed_low = normed.astype(jnp.bfloat16)
    hidden = matmul(normed_low, weight_in)
    active = swish_act(hidden).astype(jnp.bfloat16)
    return (matmul(active, weight_out), (norm_pull, normed_low, hidden, active))


def ffn_backward(grad_branch, kept_state, weight_in, weight_out):
    norm_pull, normed_low, hidden, active = kept_state
    grad_out = grad_branch.astype(jnp.bfloat16)
    grad_active = right_product(grad_out, weight_out)
    swish_value, swish_pull = jax.vjp(swish_act, hidden)
    grad_hidden = swish_pull(grad_active)[0].astype(jnp.bfloat16)
    grad_normed = right_product(grad_hidden, weight_in)
    grad_values, grad_gain = norm_pull(grad_normed)
    return (grad_values, grad_gain[None], [(normed_low, grad_hidden)], [(active, grad_out)])


TABLE = 2 * FRAMES
SCALE = HEAD_DIM ** (-0.5)


def nn(left_side, right_side):
    return lax.dot_general(
        left_side, right_side, (((1,), (0,)), ((), ())), preferred_element_type=jnp.float32
    )


def attend_kernel(q_ref, k_ref, v_ref, bias_ref, pos_ref, allow_ref, mixed_ref, prob_ref):
    query = q_ref[...].astype(jnp.float32)
    query_u = ((query + bias_ref[0:1, :]) * SCALE).astype(jnp.bfloat16)
    query_v = ((query + bias_ref[1:2, :]) * SCALE).astype(jnp.bfloat16)
    table = right_product(query_v, pos_ref[...])
    for m in range(MICRO):
        rows = slice(m * FRAMES, (m + 1) * FRAMES)
        content = right_product(query_u[rows], k_ref[rows, :])
        moved = pltpu.roll(table[rows], TABLE - FRAMES + 1, 1, stride=1, stride_axis=0)
        scores = jnp.where(allow_ref[m] > 0, content + moved[:, :FRAMES], -1e30)
        weight = jnp.exp(scores - jnp.max(scores, axis=-1, keepdims=True))
        prob = (weight / jnp.sum(weight, axis=-1, keepdims=True)).astype(jnp.bfloat16)
        prob_ref[m, 0] = prob
        mixed_ref[rows, :] = nn(prob, v_ref[rows, :]).astype(jnp.bfloat16)


def attend_back_kernel(
    q_ref, k_ref, v_ref, bias_ref, pos_ref, prob_ref, grad_ref, dq_ref, dk_ref, dv_ref, dpos_ref, dbias_ref
):
    query = q_ref[...].astype(jnp.float32)
    query_u = ((query + bias_ref[0:1, :]) * SCALE).astype(jnp.bfloat16)
    query_v = ((query + bias_ref[1:2, :]) * SCALE).astype(jnp.bfloat16)
    across = lax.broadcasted_iota(jnp.int32, (FRAMES, FRAMES), 0)
    down = lax.broadcasted_iota(jnp.int32, (FRAMES, FRAMES), 1)
    swap = jnp.where(across + down == FRAMES - 1, 1.0, 0.0).astype(jnp.bfloat16)
    tables, grads_u = [], []
    for m in range(MICRO):
        rows = slice(m * FRAMES, (m + 1) * FRAMES)
        prob = prob_ref[m, 0]
        grad = grad_ref[rows, :]
        dv_ref[rows, :] = left_product(prob, grad).astype(jnp.bfloat16)
        grad_prob = right_product(grad, v_ref[rows, :])
        wide = prob.astype(jnp.float32)
        inner = jnp.sum(wide * grad_prob, axis=-1, keepdims=True)
        grad_score = wide * (grad_prob - inner)
        low = grad_score.astype(jnp.bfloat16)
        grads_u.append(nn(low, k_ref[rows, :]))
        dk_ref[rows, :] = left_product(low, query_u[rows]).astype(jnp.bfloat16)
        turned = nn(low, swap)
        padded = jnp.concatenate([turned, jnp.zeros_like(turned)], axis=1)
        tables.append(pltpu.roll(padded, 0, 1, stride=1, stride_axis=0))
    table = jnp.concatenate(tables, axis=0).astype(jnp.bfloat16)
    grad_u = jnp.concatenate(grads_u, axis=0) * SCALE
    grad_v = nn(table, pos_ref[...]) * SCALE
    dpos_ref[...] = left_product(table, query_v).astype(jnp.bfloat16)
    dq_ref[...] = (grad_u + grad_v).astype(jnp.bfloat16)
    dbias_ref[0:1, :] = jnp.sum(grad_u, axis=0, keepdims=True)
    dbias_ref[1:2, :] = jnp.sum(grad_v, axis=0, keepdims=True)


def head_spec(rows, offset=0):
    return pl.BlockSpec((rows, HEAD_DIM), lambda h: (0, offset + h))


PROB_SPEC = pl.BlockSpec((MICRO, 1, FRAMES, FRAMES), lambda h: (0, h, 0, 0))


def attend(project, bias, positions, allowed):
    rows = project.shape[0]
    return pl.pallas_call(
        attend_kernel,
        grid=(HEADS,),
        out_shape=[
            jax.ShapeDtypeStruct((rows, D), jnp.bfloat16),
            jax.ShapeDtypeStruct((MICRO, HEADS, FRAMES, FRAMES), jnp.bfloat16),
        ],
        in_specs=[
            head_spec(rows),
            head_spec(rows, HEADS),
            head_spec(rows, 2 * HEADS),
            head_spec(2),
            head_spec(TABLE),
            pl.BlockSpec((MICRO, FRAMES, FRAMES), lambda h: (0, 0, 0)),
        ],
        out_specs=[head_spec(rows), PROB_SPEC],
        name="attend",
    )(project, project, project, bias, positions, allowed)


def attend_back(project, bias, positions, prob, grad_mixed):
    rows = project.shape[0]
    wide = jax.ShapeDtypeStruct((rows, D), jnp.bfloat16)
    return pl.pallas_call(
        attend_back_kernel,
        grid=(HEADS,),
        out_shape=[
            wide,
            wide,
            wide,
            jax.ShapeDtypeStruct((TABLE, D), jnp.bfloat16),
            jax.ShapeDtypeStruct((2, D), jnp.float32),
        ],
        in_specs=[
            head_spec(rows),
            head_spec(rows, HEADS),
            head_spec(rows, 2 * HEADS),
            head_spec(2),
            head_spec(TABLE),
            PROB_SPEC,
            head_spec(rows),
        ],
        out_specs=[head_spec(rows), head_spec(rows), head_spec(rows), head_spec(TABLE), head_spec(2)],
        name="attend_back",
    )(project, project, project, bias, positions, prob, grad_mixed)


def attn_forward(values, gain_row, weight_qkv, weight_out, bias, positions, allowed):
    normed, norm_pull = jax.vjp(layer_norm, values, gain_row)
    normed_low = normed.astype(jnp.bfloat16)
    project = matmul(normed_low, weight_qkv).astype(jnp.bfloat16)
    mixed_heads, prob = attend(project, bias, positions, allowed)
    kept_state = (norm_pull, normed_low, project, prob, mixed_heads)
    return (matmul(mixed_heads, weight_out), kept_state)


def attn_backward(grad_res, kept_state, weight_qkv, weight_out, bias, positions):
    norm_pull, normed_low, project, prob, mixed_heads = kept_state
    grad_branch = grad_res.astype(jnp.bfloat16)
    grad_mixed = right_product(grad_branch, weight_out).astype(jnp.bfloat16)
    grad_q, grad_k, grad_v, grad_pos, grad_bias = attend_back(
        project, bias, positions, prob, grad_mixed
    )
    grad_project = jnp.concatenate([grad_q, grad_k, grad_v], axis=1)
    grad_normed = right_product(grad_project, weight_qkv)
    grad_values, grad_gain = norm_pull(grad_normed)
    grad_vec = jnp.concatenate([grad_gain[None], grad_bias], axis=0)
    return (grad_values, grad_vec, [(normed_low, grad_project)], [(mixed_heads, grad_branch)], grad_pos)


def conv_forward(values, gain_row, gain_inner, weight_in, weight_out, kernel_rows, tap_masks):
    normed, norm_pull = jax.vjp(layer_norm, values, gain_row)
    normed_low = normed.astype(jnp.bfloat16)
    gated = matmul(normed_low, weight_in)
    active, inner_pull = jax.vjp(
        partial(conv_inner, tap_masks=tap_masks), gated, gain_inner, kernel_rows
    )
    active_low = active.astype(jnp.bfloat16)
    return (matmul(active_low, weight_out), (norm_pull, normed_low, inner_pull, active_low))


def conv_backward(grad_res, kept_state, weight_in, weight_out):
    norm_pull, normed_low, inner_pull, active_low = kept_state
    grad_branch = grad_res.astype(jnp.bfloat16)
    grad_active = right_product(grad_branch, weight_out)
    grad_gated, grad_inner, grad_taps = inner_pull(grad_active)
    grad_gated_low = grad_gated.astype(jnp.bfloat16)
    grad_normed = right_product(grad_gated_low, weight_in)
    grad_values, grad_gain = norm_pull(grad_normed)
    grad_vec = jnp.concatenate([grad_gain[None], grad_inner[None], grad_taps], axis=0)
    return (grad_values, grad_vec, [(normed_low, grad_gated_low)], [(active_low, grad_branch)])


def other_core(d):
    return d + 1 - 2 * (d % 2)


def flip_x(d):
    return d + 2 - 4 * ((d // 2) % 2)


def flip_y(d):
    return d + 4 - 8 * ((d // 4) % 2)


def greet(peers):
    barrier = pltpu.get_barrier_semaphore()
    for peer in peers:
        pl.semaphore_signal(barrier, inc=1, device_id=peer, device_id_type=MESH)
    pl.semaphore_wait(barrier, len(peers))


def rows_of(start, count):
    return pl.ds(pl.multiple_of(start, 16), count)


def gather_kernel(n, count, *refs):
    shards = refs[: count + 1]
    fulls = refs[count + 1 : 2 * count + 2]
    send_sem, recv_sem = refs[2 * count + 2 :]
    z = lax.axis_index("fsdp")
    d = lax.axis_index("dp")
    core, place = d % 2, d // 2
    x_peer, y_peer, core_peer = {"dp": flip_x(d)}, {"dp": flip_y(d)}, {"dp": other_core(d)}
    z_peers = [{"fsdp": (z + k) % n} for k in range(1, n)]
    greet(z_peers + [x_peer, y_peer, core_peer])
    used = [0]
    started = []

    def send(src, dst, peer):
        index = used[0]
        used[0] += 1
        copy = pltpu.make_async_remote_copy(
            src_ref=src,
            dst_ref=dst,
            send_sem=send_sem.at[index],
            recv_sem=recv_sem.at[index],
            device_id=peer,
            device_id_type=MESH,
        )
        copy.start()
        started.append(copy)
        return copy

    first = {}
    for t in range(count):
        depth = shards[t].shape[0]
        part = depth // 8
        for k in range(1, n):
            first[t, k] = send(
                shards[t].at[rows_of((core * 4 + place) * part, part), :],
                fulls[t].at[rows_of(z * depth + (core * 4 + place) * part, part), :],
                z_peers[k - 1],
            )
    late = []
    small = shards[count].shape[0]
    for k in range(1, n):
        late.append(send(shards[count], fulls[count].at[rows_of(z * small, small), :], z_peers[k - 1]))
    for t in range(count + 1):
        depth = shards[t].shape[0]
        late.append(send(shards[t], fulls[t].at[rows_of(z * depth, depth), :], core_peer))

    stages = [(t, k) for t in range(count) for k in range(1, n)]
    across, corner = {}, {}

    def piece(t, k, where, half=None):
        depth = shards[t].shape[0]
        part = depth // 8
        start = ((z + n - k) % n) * depth + (core * 4 + where) * part
        if half is None:
            return fulls[t].at[rows_of(start, part), :]
        return fulls[t].at[rows_of(start + half * (part // 2), part // 2), :]

    flip_1 = place + 1 - 2 * (place % 2)
    flip_2 = place + 2 - 4 * (place // 2)
    for i in range(len(stages) + 2):
        if i < len(stages):
            t, k = stages[i]
            first[t, k].wait_recv()
            mine = piece(t, k, place)
            across[i] = (send(mine, mine, x_peer), send(mine, mine, y_peer))
        if 0 <= i - 1 < len(stages):
            t, k = stages[i - 1]
            by_x, by_y = across[i - 1]
            by_y.wait_recv()
            view = piece(t, k, flip_2, 0)
            one = send(view, view, x_peer)
            by_x.wait_recv()
            view = piece(t, k, flip_1, 1)
            corner[i - 1] = (one, send(view, view, y_peer))
        if 0 <= i - 2 < len(stages):
            t, k = stages[i - 2]
            for copy in corner[i - 2]:
                copy.wait_recv()
            depth = shards[t].shape[0]
            half = depth // 2
            view = fulls[t].at[rows_of(((z + n - k) % n) * depth + core * half, half), :]
            late.append(send(view, view, core_peer))
    for copy in late:
        copy.wait_recv()
    for copy in started:
        copy.wait_send()


def gather_all(n, shards, small, collective_id):
    count = len(shards)
    given = list(shards) + [small]
    copies = count * (n - 1) * 6 + (n - 1) + count + 1
    return pl.pallas_call(
        partial(gather_kernel, n, count),
        out_shape=[jax.ShapeDtypeStruct((n * s.shape[0], s.shape[1]), s.dtype) for s in given],
        in_specs=[pl.BlockSpec(memory_space=pltpu.HBM)] * (count + 1),
        out_specs=[pl.BlockSpec(memory_space=pltpu.HBM)] * (count + 1),
        scratch_shapes=[pltpu.SemaphoreType.DMA((copies,)), pltpu.SemaphoreType.DMA((copies,))],
        compiler_params=pltpu.CompilerParams(collective_id=collective_id, has_side_effects=True),
        name="gather_weights",
    )(*given)


def spread_kernel(count, *refs):
    pieces = refs[:count]
    wholes = refs[count : 2 * count]
    send_sem, recv_sem, own_sem = refs[2 * count :]
    d = lax.axis_index("dp")
    core, place = d % 2, d // 2
    x_peer, y_peer, core_peer = {"dp": flip_x(d)}, {"dp": flip_y(d)}, {"dp": other_core(d)}
    greet([x_peer, y_peer, core_peer])
    used = [0]
    started = []

    def send(src, dst, peer):
        index = used[0]
        used[0] += 1
        copy = pltpu.make_async_remote_copy(
            src_ref=src,
            dst_ref=dst,
            send_sem=send_sem.at[index],
            recv_sem=recv_sem.at[index],
            device_id=peer,
            device_id_type=MESH,
        )
        copy.start()
        started.append(copy)
        return copy

    flip_1 = place + 1 - 2 * (place % 2)
    flip_2 = place + 2 - 4 * (place // 2)

    def region(t, owner_core, where, half=None):
        part = pieces[t].shape[0]
        start = (owner_core * 4 + where) * part
        if half is None:
            return wholes[t].at[rows_of(start, part), :]
        return wholes[t].at[rows_of(start + half * (part // 2), part // 2), :]

    across, own, late = [], [], []
    for t in range(count):
        spot = region(t, core, place)
        across.append((send(pieces[t], spot, x_peer), send(pieces[t], spot, y_peer)))
        late.append(send(pieces[t], spot, core_peer))
        keep = pltpu.make_async_copy(pieces[t], spot, own_sem.at[t])
        keep.start()
        own.append(keep)
    corner = []
    for t in range(count):
        by_x, by_y = across[t]
        by_y.wait_recv()
        view = region(t, core, flip_2, 0)
        one = send(view, view, x_peer)
        view = region(t, core, flip_2)
        late.append(send(view, view, core_peer))
        by_x.wait_recv()
        view = region(t, core, flip_1, 1)
        corner.append((one, send(view, view, y_peer)))
        view = region(t, core, flip_1)
        late.append(send(view, view, core_peer))
    for t in range(count):
        for copy in corner[t]:
            copy.wait_recv()
        view = region(t, core, 3 - place)
        late.append(send(view, view, core_peer))
    for copy in own:
        copy.wait()
    for copy in late:
        copy.wait_recv()
    for copy in started:
        copy.wait_send()


def spread_all(pieces, collective_id):
    count = len(pieces)
    return pl.pallas_call(
        partial(spread_kernel, count),
        out_shape=[jax.ShapeDtypeStruct((8 * s.shape[0], s.shape[1]), s.dtype) for s in pieces],
        in_specs=[pl.BlockSpec(memory_space=pltpu.VMEM)] * count,
        out_specs=[pl.BlockSpec(memory_space=pltpu.HBM)] * count,
        scratch_shapes=[
            pltpu.SemaphoreType.DMA((8 * count,)),
            pltpu.SemaphoreType.DMA((8 * count,)),
            pltpu.SemaphoreType.DMA((count,)),
        ],
        compiler_params=pltpu.CompilerParams(collective_id=collective_id, has_side_effects=True),
        name="spread_sums",
    )(*pieces)


def add_rows(dst, dst_row, src, src_row, count):
    @pl.loop(0, count // 16)
    def _(step):
        at = pl.ds(pl.multiple_of(dst_row + step * 16, 16), 16)
        take = pl.ds(pl.multiple_of(src_row + step * 16, 16), 16)
        total = dst[at, :].astype(jnp.float32) + src[take, :].astype(jnp.float32)
        dst[at, :] = total.astype(jnp.bfloat16)


def sums_kernel(n, plan, small, *refs):
    count = len(plan)
    inputs = sum(2 * len(widths) for _, widths in plan)
    operands = list(refs[:inputs])
    refs = refs[inputs:]
    if small:
        small_ref, refs = refs[0], refs[1:]
    outs, refs = refs[:count], refs[count:]
    if small:
        small_out, refs = refs[0], refs[1:]
    held, refs = refs[:count], refs[count:]
    from_core, refs = refs[:count], refs[count:]
    from_first, refs = refs[:count], refs[count:]
    from_second, refs = refs[:count], refs[count:]
    from_z, refs = refs[:count], refs[count:]
    if small:
        (small_held, small_got, small_z), refs = refs[:3], refs[3:]
    send_sem, recv_sem = refs
    pairs = []
    for _, widths in plan:
        pairs.append([(operands.pop(0), operands.pop(0)) for _ in widths])
    z = lax.axis_index("fsdp")
    d = lax.axis_index("dp")
    core, place = d % 2, d // 2
    x_bit, y_bit = place % 2, place // 2
    peers = [{"dp": flip_x(d)}, {"dp": flip_y(d)}]
    core_peer = {"dp": other_core(d)}
    z_peers = [{"fsdp": (z + k) % n} for k in range(1, n)]
    greet(z_peers + peers + [core_peer])
    used = [0]
    started = []

    def send(src, dst, peer, keep=True):
        index = used[0]
        used[0] += 1
        copy = pltpu.make_async_remote_copy(
            src_ref=src,
            dst_ref=dst,
            send_sem=send_sem.at[index],
            recv_sem=recv_sem.at[index],
            device_id=peer,
            device_id_type=MESH,
        )
        copy.start()
        if keep:
            started.append(copy)
        return copy

    units = [(t, k) for t in range(count) for k in [*range(1, n), 0]]
    part = [rows // (8 * n) for rows, _ in plan]
    arrive, first, second, third = {}, {}, {}, {}

    def make(t, k, spare):
        half = 4 * part[t]
        tile = 128 * 1024 // half
        column = ((z + k) % n) * 2 * half
        offset = 0
        for (left, right), width in zip(pairs[t], plan[t][1]):
            tiles = width // tile

            @pl.loop(0, 2 * tiles)
            def _(step):
                own, index = step // tiles, step % tiles
                side = own * core + (1 - own) * (1 - core)
                source = pl.ds(pl.multiple_of(column + side * half, 128), half)
                row = own * (k * half) + (1 - own) * ((n + spare) * half)
                across = pl.ds(pl.multiple_of(index * tile, 128), tile)
                target = pl.ds(pl.multiple_of(offset + index * tile, 128), tile)
                block = left_product(left[:, source], right[:, across])
                held[t][rows_of(row, half), target] = block.astype(jnp.bfloat16)

            offset += width

    for i in range(len(units) + 6):
        if i < len(units):
            t, k = units[i]
            half, spare = 4 * part[t], i % 2
            if i >= 2 and units[i - 2][0] == t:
                arrive[i - 2].wait_send()
            make(t, k, spare)
            arrive[i] = send(
                held[t].at[pl.ds((n + spare) * half, half), :],
                from_core[t].at[pl.ds(k * half, half), :],
                core_peer,
                keep=i + 2 >= len(units) or units[i + 2][0] != t,
            )
        if small and i < 3:
            if i == 0:
                small_held[...] = small_ref[...]
            else:
                small_copy.wait()
                small_held[...] += small_got[i - 1]
            small_copy = send(small_held, small_got.at[i], [core_peer, *peers][i], keep=False)
        if small and i == 3:
            small_copy.wait()
            small_held[...] += small_got[2]
            width = small_out.shape[1]
            small_z_copies = [
                send(
                    small_held.at[:, pl.ds(pl.multiple_of(((z + k) % n) * width, 128), width)],
                    small_z.at[k - 1],
                    z_peers[k - 1],
                )
                for k in range(1, n)
            ]
        j = i - 1
        if 0 <= j < len(units):
            t, k = units[j]
            p, base = part[t], k * 4 * part[t]
            arrive[j].wait_recv()
            add_rows(held[t], base, from_core[t], base, 4 * p)
            if j % 2 == 0:
                first[j] = [
                    send(
                        held[t].at[rows_of(base + (2 * y + 1 - x_bit) * p, p), :],
                        from_first[t].at[pl.ds((2 * k + y) * p, p), :],
                        peers[0],
                    )
                    for y in range(2)
                ]
            else:
                first[j] = [
                    send(
                        held[t].at[rows_of(base + 2 * (1 - y_bit) * p, 2 * p), :],
                        from_first[t].at[pl.ds(2 * k * p, 2 * p), :],
                        peers[1],
                    )
                ]
        j = i - 3
        if 0 <= j < len(units):
            t, k = units[j]
            p, base = part[t], k * 4 * part[t]
            for copy in first[j]:
                copy.wait_recv()
            if j % 2 == 0:
                for y in range(2):
                    add_rows(held[t], base + (2 * y + x_bit) * p, from_first[t], (2 * k + y) * p, p)
                gone, peer = base + (2 * (1 - y_bit) + x_bit) * p, peers[1]
            else:
                add_rows(held[t], base + 2 * y_bit * p, from_first[t], 2 * k * p, 2 * p)
                gone, peer = base + (2 * y_bit + 1 - x_bit) * p, peers[0]
            second[j] = send(held[t].at[rows_of(gone, p), :], from_second[t].at[pl.ds(k * p, p), :], peer)
        j = i - 5
        if 0 <= j < len(units):
            t, k = units[j]
            p, base = part[t], k * 4 * part[t]
            second[j].wait_recv()
            add_rows(held[t], base + place * p, from_second[t], k * p, p)
            if k > 0:
                third[t, k] = send(
                    held[t].at[rows_of(base + place * p, p), :],
                    from_z[t].at[pl.ds((k - 1) * p, p), :],
                    z_peers[k - 1],
                )
    for t in range(count):
        p = part[t]
        for k in range(1, n):
            third[t, k].wait_recv()

        @pl.loop(0, p // 16)
        def _(step):
            total = held[t][pl.ds(pl.multiple_of(place * p + step * 16, 16), 16), :].astype(jnp.float32)
            for k in range(1, n):
                at = pl.ds(pl.multiple_of((k - 1) * p + step * 16, 16), 16)
                total = total + from_z[t][at, :].astype(jnp.float32)
            outs[t][pl.ds(pl.multiple_of(step * 16, 16), 16), :] = total.astype(jnp.bfloat16)

    if small:
        for copy in small_z_copies:
            copy.wait_recv()
        total = small_held[:, pl.ds(pl.multiple_of(z * width, 128), width)]
        for k in range(1, n):
            total = total + small_z[k - 1]
        small_out[...] = total
    for copy in started:
        copy.wait_send()


def sum_products(n, tensors, small, collective_id):
    plan = [
        (pairs[0][0].shape[1], tuple(right.shape[1] for _, right in pairs)) for pairs in tensors
    ]
    count = len(plan)
    operands = [side for pairs in tensors for pair in pairs for side in pair]
    shapes = [(rows, sum(widths)) for rows, widths in plan]
    out_shape = [jax.ShapeDtypeStruct((r // (8 * n), c), jnp.bfloat16) for r, c in shapes]

    def room(over, under):
        return [pltpu.VMEM((r * over // under, c), jnp.bfloat16) for r, c in shapes]

    scratch = [
        *room(n + 2, 2 * n),
        *room(1, 2),
        *room(1, 4),
        *room(1, 8),
        *room(n - 1, 8 * n),
    ]
    copies = count * (5 * n - 1)
    if small is not None:
        operands.append(small)
        depth, width = small.shape
        out_shape.append(jax.ShapeDtypeStruct((depth, width // n), jnp.float32))
        scratch += [
            pltpu.VMEM((depth, width), jnp.float32),
            pltpu.VMEM((3, depth, width), jnp.float32),
            pltpu.VMEM((n - 1, depth, width // n), jnp.float32),
        ]
        copies += 3 + n - 1
    whole = pl.BlockSpec(memory_space=pltpu.VMEM)
    return pl.pallas_call(
        partial(sums_kernel, n, plan, small is not None),
        out_shape=out_shape,
        in_specs=[whole] * len(operands),
        out_specs=[whole] * len(out_shape),
        scratch_shapes=[
            *scratch,
            pltpu.SemaphoreType.DMA((copies,)),
            pltpu.SemaphoreType.DMA((copies,)),
        ],
        compiler_params=pltpu.CompilerParams(
            collective_id=collective_id, has_side_effects=True, vmem_limit_bytes=63 * 1024 * 1024
        ),
        name="sum_products",
    )(*operands)


EARLY = (6, 7, 4, 5, 3)
LATE = (2, 0, 1)


def fallback_reduce(pairs):
    grad = jnp.concatenate([left_product(left, right) for left, right in pairs], axis=1)
    part = lax.psum_scatter(grad.astype(jnp.bfloat16), "fsdp", scatter_dimension=0, tiled=True)
    return lax.psum(part, "dp")


def on_device(
    fast,
    n,
    inputs,
    cotangent,
    lengths,
    buckets,
    ffn1_in,
    ffn1_out,
    attn_in,
    attn_out,
    conv_in,
    conv_out,
    ffn2_in,
    ffn2_out,
    norm_gains,
    pos_bias,
    kernel,
):
    shards = [ffn1_in, ffn1_out, attn_in, attn_out, conv_in, conv_out, ffn2_in, ffn2_out]
    width = norm_gains.shape[1]
    vectors = jnp.concatenate(
        [norm_gains, pos_bias, kernel, jnp.zeros((3, width), norm_gains.dtype)], axis=0
    )
    if fast:
        gathered = gather_all(n, shards, vectors, 0)
        weights, vec = gathered[:8], gathered[8]
        vec = vec.reshape(n, 16, width).transpose(1, 0, 2).reshape(16, D)
    else:
        weights = [lax.all_gather(s, "fsdp", axis=0, tiled=True) for s in shards]
        vec = lax.all_gather(vectors, "fsdp", axis=1, tiled=True)
    vec = vec.astype(jnp.float32)
    gains, biases, taps = vec[0:6], vec[6:8], vec[8:13]
    plans = [frame_plan(lengths[m], buckets[m]) for m in range(MICRO)]
    allowed = jnp.stack([p[0] for p in plans], axis=0).astype(jnp.float32)
    tap_masks = jnp.concatenate([p[1] for p in plans], axis=1)
    table_low = sinusoid(1).astype(jnp.bfloat16)
    mirror_low = sinusoid(-1).astype(jnp.bfloat16)

    stream = inputs.astype(jnp.float32)
    branch, kept_one = ffn_forward(stream, gains[0], weights[0], weights[1])
    section_one = stream + 0.5 * branch
    positions = matmul(table_low, weights[2][:, 3 * D :]).astype(jnp.bfloat16)
    mirrored = matmul(mirror_low, weights[2][:, 3 * D :]).astype(jnp.bfloat16)
    weight_qkv = weights[2][:, : 3 * D]
    branch, kept_two = attn_forward(
        section_one, gains[1], weight_qkv, weights[3], biases, positions, allowed
    )
    section_two = section_one + branch
    branch, kept_three = conv_forward(
        section_two, gains[2], gains[3], weights[4], weights[5], taps, tap_masks
    )
    section_three = section_two + branch
    branch, kept_four = ffn_forward(section_three, gains[4], weights[6], weights[7])
    section_four = section_three + 0.5 * branch
    final_out, final_pull = jax.vjp(layer_norm, section_four, gains[5])
    grad_stream, grad_final = final_pull(cotangent.astype(jnp.float32))

    grad_values, grad_vec4, grad_in4, grad_out4 = ffn_backward(
        0.5 * grad_stream, kept_four, weights[6], weights[7]
    )
    sums = [None] * 8
    grad_stream = grad_stream + grad_values
    grad_values, grad_vec3, grad_in3, grad_out3 = conv_backward(
        grad_stream, kept_three, weights[4], weights[5]
    )
    grad_stream = grad_stream + grad_values
    grad_values, grad_vec2, grad_in2, grad_out2, grad_pos = attn_backward(
        grad_stream, kept_two, weight_qkv, weights[3], biases, mirrored
    )
    grad_stream = grad_stream + grad_values
    grad_values, grad_vec1, grad_in1, grad_out1 = ffn_backward(
        0.5 * grad_stream, kept_one, weights[0], weights[1]
    )
    grad_in2 = grad_in2 + [(mirror_low, grad_pos)]
    grad_stream = grad_stream + grad_values

    grad_vectors = jnp.concatenate(
        [
            grad_vec1,
            grad_vec2[0:1],
            grad_vec3[0:2],
            grad_vec4,
            grad_final[None],
            grad_vec2[1:3],
            grad_vec3[2:7],
            jnp.zeros((3, D), jnp.float32),
        ],
        axis=0,
    )
    tensors = [grad_in1, grad_out1, grad_in2, grad_out2, grad_in3, grad_out3, grad_in4, grad_out4]
    if fast:
        early = sum_products(n, [tensors[i] for i in EARLY], None, 2)
        *late, grad_small = sum_products(n, [tensors[i] for i in LATE], grad_vectors, 3)
        for index, total in zip(EARLY + LATE, list(early) + late):
            sums[index] = total
        sums = spread_all(sums, 1)
    else:
        sums = [fallback_reduce(pairs) for pairs in tensors]
        grad_small = lax.psum(
            lax.psum_scatter(grad_vectors, "fsdp", scatter_dimension=1, tiled=True), "dp"
        )
    grads = [s.astype(jnp.float32) for s in sums]
    return (
        final_out.astype(jnp.bfloat16),
        grad_stream,
        *grads,
        grad_small[0:6],
        grad_small[6:8],
        grad_small[8:13],
    )


def solution(mesh):
    in_specs = (
        P(("dp", "fsdp"), None),
        P(("dp", "fsdp"), None),
        P(("dp", "fsdp"), None),
        P(("dp", "fsdp")),
        P("fsdp", None),
        P("fsdp", None),
        P("fsdp", None),
        P("fsdp", None),
        P("fsdp", None),
        P("fsdp", None),
        P("fsdp", None),
        P("fsdp", None),
        P(None, "fsdp"),
        P(None, "fsdp"),
        P(None, "fsdp"),
    )
    out_specs = (
        P(("dp", "fsdp"), None),
        P(("dp", "fsdp"), None),
        P("fsdp", None),
        P("fsdp", None),
        P("fsdp", None),
        P("fsdp", None),
        P("fsdp", None),
        P("fsdp", None),
        P("fsdp", None),
        P("fsdp", None),
        P(None, "fsdp"),
        P(None, "fsdp"),
        P(None, "fsdp"),
    )
    sizes = dict(mesh.shape)
    n = sizes["fsdp"]
    fast = sizes["dp"] == 8 and n == 4
    return jax.shard_map(
        partial(on_device, fast, n), mesh=mesh, in_specs=in_specs, out_specs=out_specs, check_vma=False
    )
```

profile of v0, /device:TPU:0, one launch (start us, length us, event | category | flops | bytes accessed | tf_op | source)
XLA Modules:
  0.0 713.6 jit_solution(5594175677511254699)
XLA Ops:
  0.7 1.4 maximum_maximum_fusion.refs_8_
  2.1 196.0 %gather_weights.1 = (bf16[1024,4096]{1,0:T(8,128)(2,1)}, bf16[4096,1024]{1,0:T(8,128)(2,1)}, bf16[1024,4096]{1,0:T(8,128)(2,1)}, bf16[1024,1024]{1,0:T(8,128)(2,...) custom-call(bf16[256,4096]{1,0:T(8,128)(2,1)} %refs_0_.1, ...), custom_call_target="tpu_custom_call" | custom-call | tf_op jit(solution)/shard_map/gather_weights/pallas_call | solution.py:405
  198.2 0.8 copy.43
  200.7 9.9 %multiply_convert_fusion.1 = (bf16[384,4096]{1,0:T(8,128)(2,1)S(1)}, f32[384,4096]{1,0:T(8,128)}) fusion(bf16[384,1024]{1,0:T(8,128)(2,1)S(1)} %fusion.25.refs_4_, bf16[1024,4096]{1,0:T(8,128)(2,1)} %get-tuple-element.55), kind=kOutput, calls=%fused_computation.10 | convolution fusion | flops 3229089792 | bytes 18612224 | tf_op jit(solution)/shard_map/dot_general | solution.py:24
  210.6 3.6 fusion.103
  214.5 0.8 copy-done.62
  215.7 3.9 fusion.10.q_ref.k_ref.v_ref
  222.3 0.8 add_convert_fusion.3.allow_ref
  223.1 1.2 fusion.50
  224.3 0.8 multiply_cosine_fusion
  225.3 3.5 fusion.41.pos_ref
  228.8 0.6 copy.32
  229.4 10.2 %attend.1 = (bf16[384,1024]{1,0:T(8,128)(2,1)}, bf16[2,8,192,192]{3,2,1,0:T(8,128)(2,1)}) custom-call(bf16[384,3072]{1,0:T(8,128)(2,1)} %fusion.10.q_ref.k_ref.v_ref, bf16[384,3072]{1,0:T(8,128)(2,1)} %fusion.10.q_ref.k_ref.v_ref, bf16[384,3072]{1,0:T(8,128)(2,1)} %fusion.10.q_ref.k_ref.v_ref, f32[2,1024]{1,0:T(2,128)} %bitcast.105, ...), custom_call_target="tpu_custom_call" | custom-call | tf_op jit(solution)/shard_map/attend/pallas_call | solution.py:197
  239.6 3.0 fusion.104
  243.8 1.8 fusion.107
  246.0 1.9 fusion.92
  248.0 1.9 fusion.93
  251.9 4.6 fusion.91
  257.4 0.7 copy-done.73
  258.1 0.8 copy-done.5
  258.9 1.1 fusion.105
  260.6 6.4 multiply_convert_fusion
  267.1 3.6 fusion.106
  271.0 0.8 copy-done.33
  271.8 1.1 fusion.28
  273.0 1.5 fusion.90
  274.7 11.1 %fusion.2.refs_1_ = bf16[384,4096]{1,0:T(8,128)(2,1)S(1)} fusion(f32[384,4096]{1,0:T(8,128)} %get-tuple-element.198, bf16[384,1024]{1,0:T(8,128)(2,1)S(1)} %multiply_convert_fusion.3.refs_3_, bf16[4096,1024]{1,0:T(8,128)(2,1)} %get-tuple-element.67), kind=kOutput, calls=%fused_computation.4 | convolution fusion | flops 3236954112 | bytes 18612224 | tf_op jit(solution)/shard_map/dot_general | solution.py:34
  285.8 7.9 %multiply_reduce_fusion.5 = (f32[1024]{0:T(1024)}, f32[384]{0:T(512)S(1)}, f32[384,1024]{1,0:T(8,128)S(1)}) fusion(f32[384,1024]{1,0:T(8,128)S(1)} %get-tuple-element.196, f32[384]{0:T(512)S(1)} %fusion.75, f32[384]{0:T(512)S(1)} %broadcast_multiply_fusion.1, f32[1024]{0:T(1024)S(1)} %bitcast.131, bf16[384,4096]{1,0:T(8,128)(2,1)S(1)} %fusion.2.refs_1_, ...), kind=kOutput, calls=%fused_computation.69 | convolution fusion | flops 3223976448 | bytes 14692864 | tf_op jit(solution)/shard_map/dot_general | solution.py:34
  294.6 2.1 copy-done.74
  296.7 2.3 multiply_reduce_fusion.6
  299.6 0.8 copy-done.10
  301.4 2.7 multiply_reduce_fusion.4
  305.0 1.4 fusion.33
  307.1 2.0 copy-done.72
  309.1 2.6 multiply_reduce_fusion.7
  312.3 1.1 copy-done.8
  313.4 1.1 fusion.47.refs_9_
  314.5 132.8 %sum_products.3 = (bf16[32,4096]{1,0:T(8,128)(2,1)}, bf16[128,1024]{1,0:T(8,128)(2,1)}, bf16[32,2048]{1,0:T(8,128)(2,1)}, bf16[32,1024]{1,0:T(8,128)(2,1)}, bf16[32,1024]{1,0:T(8,128)(2,1)}) custom-call(bf16[384,1024]{1,0:T(8,128)(2,1)} %copy-done.26, bf16[384,4096]{1,0:T(8,128)(2,1)} %copy-done.31, bf16[384,4096]{1,0:T(8,128)(2,1)} %copy-done.30, ...), custom_call_target="tpu_custom_call" | custom-call | tf_op jit(solution)/shard_map/sum_products/pallas_call | solution.py:721
  447.3 0.8 pad_add_fusion.1
  448.1 3.5 convolution_convert_fusion.grad_ref
  451.8 0.9 copy-done.28
  452.7 3.5 fusion.44.pos_ref
  456.2 12.1 %attend_back.1 = (bf16[384,1024]{1,0:T(8,128)(2,1)}, bf16[384,1024]{1,0:T(8,128)(2,1)}, bf16[384,1024]{1,0:T(8,128)(2,1)}, bf16[384,1024]{1,0:T(8,128)(2,1)}, f32[2,1024]{1,0:T(2,128)}) custom-call(bf16[384,3072]{1,0:T(8,128)(2,1)} %fusion.10.q_ref.k_ref.v_ref, bf16[384,3072]{1,0:T(8,128)(2,1)} %fusion.10.q_ref.k_ref.v_ref, ...), custom_call_target="tpu_custom_call" | custom-call | tf_op jit(solution)/shard_map/attend_back/pallas_call | solution.py:220
  468.4 1.3 constant_dynamic-update-slice_fusion.2
  470.0 1.2 copy-done.3
  471.2 5.9 multiply_reduce_fusion.8
  477.8 0.8 copy-done.7
  479.1 1.5 multiply_convert_fusion.2
  480.6 11.1 %fusion.5.refs_5_ = bf16[384,4096]{1,0:T(8,128)(2,1)S(1)} fusion(f32[384,4096]{1,0:T(8,128)} %get-tuple-element.190, bf16[384,1024]{1,0:T(8,128)(2,1)S(1)} %get-tuple-element.118.refs_7_, bf16[4096,1024]{1,0:T(8,128)(2,1)} %get-tuple-element.56), kind=kOutput, calls=%fused_computation.7 | convolution fusion | flops 3236954112 | bytes 18612224 | tf_op jit(solution)/shard_map/dot_general | solution.py:34
  491.8 7.4 %fusion.30 = (f32[384]{0:T(512)S(1)}, f32[384,1024]{1,0:T(8,128)S(1)}) fusion(bf16[384,1024]{1,0:T(8,128)(2,1)S(1)} %copy-done.1, f32[1024]{0:T(1024)S(1)} %bitcast.108, f32[384]{0:T(512)S(1)} %copy-done.48, bf16[384,4096]{1,0:T(8,128)(2,1)S(1)} %fusion.5.refs_5_, bf16[1024,4096]{1,0:T(8,128)(2,1)} %get-tuple-element.55), kind=kOutput, calls=%fused_computation.48 | convolution fusion | flops 3223191040 | bytes 13900800 | tf_op jit(solution)/shard_map/dot_general | solution.py:34
  499.3 1.0 copy-done.15
  500.4 0.8 fusion.26
  501.2 1.3 concatenate.179.refs_8_
  502.5 131.7 %sum_products.2 = (bf16[32,4096]{1,0:T(8,128)(2,1)}, bf16[32,4096]{1,0:T(8,128)(2,1)}, bf16[128,1024]{1,0:T(8,128)(2,1)}, f32[16,256]{1,0:T(8,128)}) custom-call(bf16[384,1024]{1,0:T(8,128)(2,1)} %copy-done.23, bf16[384,3072]{1,0:T(8,128)(2,1)} %copy-done.18, bf16[384,1024]{1,0:T(8,128)(2,1)} %bitcast.101, bf16[384,1024]{1,0:T(8,128)(2,1)} %get-tuple-element.76.refs_3_, ...), custom_call_target="tpu_custom_call" | custom-call | tf_op jit(solution)/shard_map/sum_products/pallas_call | solution.py:721
  634.2 57.5 %spread_sums.1 = (bf16[256,4096]{1,0:T(8,128)(2,1)}, bf16[1024,1024]{1,0:T(8,128)(2,1)}, bf16[256,4096]{1,0:T(8,128)(2,1)}, bf16[256,1024]{1,0:T(8,128)(2,1)}, b...) custom-call(bf16[32,4096]{1,0:T(8,128)(2,1)} %get-tuple-element.78.r, ...), custom_call_target="tpu_custom_call" | custom-call | tf_op jit(solution)/shard_map/spread_sums/pallas_call | solution.py:488
  691.7 4.2 convert_element_type.266
  695.9 2.5 convert_element_type.267
  698.4 2.5 convert_element_type.268
  700.9 2.5 convert_element_type.272
  703.4 2.5 convert_element_type.273
  705.9 1.6 convert_element_type.270
  707.5 1.1 convert_element_type.269
  708.6 1.1 convert_element_type.271
  711.4 1.7 add_add_fusion.6
  (271 shorter events, 17.5 us)
Async XLA Ops:
  2.1 196.9 %copy-start = (bf16[384,1024]{1,0:T(8,128)(2,1)S(1)}, bf16[384,1024]{1,0:T(8,128)(2,1)}, u32[]{:S(2)}) copy-start(bf16[384,1024]{1,0:T(8,128)(2,1)} %param.15) | copy-start | bytes 2359300
  200.1 10.5 %slice-start = ((s8[8388608]{0:T(1024)(128)(4,1)}), s8[4194304]{0:T(1024)(128)(4,1)S(1)}, s32[]{:S(2)}) async-start(s8[8388608]{0:T(1024)(128)(4,1)} %bitcast.155), calls=%async_computation | async-start | bytes 8388608
  200.1 15.5 %slice-start.2 = ((s8[8388608]{0:T(1024)(128)(4,1)}), s8[4194304]{0:T(1024)(128)(4,1)S(1)}, s32[]{:S(2)}) async-start(s8[8388608]{0:T(1024)(128)(4,1)} %bitcast.157), calls=%async_computation.2 | async-start | bytes 8388608
  200.7 9.9 %copy-start.22 = (bf16[384,1024]{1,0:T(8,128)(2,1)}, bf16[384,1024]{1,0:T(8,128)(2,1)S(1)}, u32[]{:S(2)}) copy-start(bf16[384,1024]{1,0:T(8,128)(2,1)S(1)} %fusion.25.refs_4_) | copy-start | bytes 2359300
  200.7 9.9 %slice-start.1 = ((s8[8388608]{0:T(1024)(128)(4,1)}), s8[4194304]{0:T(1024)(128)(4,1)S(1)}, s32[]{:S(2)}) async-start(s8[8388608]{0:T(1024)(128)(4,1)} %bitcast.155), calls=%async_computation.1 | async-start | bytes 8388608
  200.7 15.0 %slice-start.3 = ((s8[8388608]{0:T(1024)(128)(4,1)}), s8[4194304]{0:T(1024)(128)(4,1)S(1)}, s32[]{:S(2)}) async-start(s8[8388608]{0:T(1024)(128)(4,1)} %bitcast.157), calls=%async_computation.3 | async-start | bytes 8388608
  210.6 3.6 copy-start.29
  214.2 25.4 %copy-start.2 = (f32[384,1024]{1,0:T(8,128)}, f32[384,1024]{1,0:T(8,128)S(1)}, u32[]{:S(2)}) copy-start(f32[384,1024]{1,0:T(8,128)S(1)} %get-tuple-element.192) | copy-start | bytes 4718596
  215.3 4.2 copy-start.58
  215.3 4.2 copy-start.49
  215.6 3.9 copy-start.23
  215.7 3.9 copy-start.69
  215.7 5.3 copy-start.70
  239.6 4.2 copy-start.71
  243.8 1.8 copy-start.24
  251.9 8.7 %slice-start.4 = ((s8[8388608]{0:T(1024)(128)(4,1)}), s8[4194304]{0:T(1024)(128)(4,1)S(1)}, s32[]{:S(2)}) async-start(s8[8388608]{0:T(1024)(128)(4,1)} %bitcast.159), calls=%async_computation.4 | async-start | bytes 8388608
  256.5 1.6 copy-start.73
  256.8 2.1 copy-start.5
  256.8 3.8 slice-start.5
  257.4 2.5 copy-start.25
  260.0 7.1 slice-start.6
  260.6 6.4 copy-start.26
  260.6 6.4 slice-start.7
  267.0 3.6 copy-start.30
  274.7 11.1 %copy-start.27 = (bf16[384,1024]{1,0:T(8,128)(2,1)}, bf16[384,1024]{1,0:T(8,128)(2,1)S(1)}, u32[]{:S(2)}) copy-start(bf16[384,1024]{1,0:T(8,128)(2,1)S(1)} %multiply_convert_fusion.3.refs_3_) | copy-start | bytes 2359300
  285.8 7.9 %copy-start.31 = (bf16[384,4096]{1,0:T(8,128)(2,1)}, bf16[384,4096]{1,0:T(8,128)(2,1)S(1)}, u32[]{:S(2)}) copy-start(bf16[384,4096]{1,0:T(8,128)(2,1)S(1)} %fusion.2.refs_1_) | copy-start | bytes 9437188
  294.3 2.4 copy-start.74
  294.6 4.4 copy-start.19
  294.6 17.7 %copy-start.6 = (f32[384,1024]{1,0:T(8,128)}, f32[384,1024]{1,0:T(8,128)S(1)}, u32[]{:S(2)}) copy-start(f32[384,1024]{1,0:T(8,128)S(1)} %get-tuple-element.130) | copy-start | bytes 4718596
  296.7 2.9 copy-start.13
  299.0 1.9 copy-start.11
  299.0 2.3 copy-start.12
  306.9 2.2 copy-start.72
  309.1 2.6 copy-start.14
  314.5 133.6 %copy-start.21 = (bf16[384,1024]{1,0:T(8,128)(2,1)S(1)}, bf16[384,1024]{1,0:T(8,128)(2,1)}, u32[]{:S(2)}) copy-start(bf16[384,1024]{1,0:T(8,128)(2,1)} %fusion.47.refs_9_) | copy-start | bytes 2359300
  448.1 3.5 copy-start.43
  448.1 3.5 copy-start.44
  468.4 1.6 copy-start.39
  471.2 6.0 copy-start.18
  471.2 6.0 copy-start.63
  477.2 1.9 copy-start.9
  477.2 1.9 copy-start.57
  480.6 11.1 %copy-start.20 = (bf16[384,1024]{1,0:T(8,128)(2,1)}, bf16[384,1024]{1,0:T(8,128)(2,1)S(1)}, u32[]{:S(2)}) copy-start(bf16[384,1024]{1,0:T(8,128)(2,1)S(1)} %get-tuple-element.118.refs_7_) | copy-start | bytes 2359300
  480.6 11.1 %copy-start.1 = (bf16[384,1024]{1,0:T(8,128)(2,1)S(1)}, bf16[384,1024]{1,0:T(8,128)(2,1)}, u32[]{:S(2)}) copy-start(bf16[384,1024]{1,0:T(8,128)(2,1)} %param.15) | copy-start | bytes 2359300
  480.6 11.2 %copy-start.46 = (f32[1,2,4,128]{3,1,2,0:T(2,128)S(1)}, f32[1,2,4,128]{3,1,2,0:T(2,128)}, u32[]{:S(2)}) copy-start(f32[1,2,4,128]{3,1,2,0:T(2,128)} %copy-done.45) | copy-start | bytes 12292
  480.6 11.2 %copy-start.48 = (f32[384]{0:T(512)S(1)}, f32[384]{0:T(512)}, u32[]{:S(2)}) copy-start(f32[384]{0:T(512)} %copy-done.47) | copy-start | bytes 4612
  491.8 7.4 %copy-start.32 = (bf16[384,4096]{1,0:T(8,128)(2,1)}, bf16[384,4096]{1,0:T(8,128)(2,1)S(1)}, u32[]{:S(2)}) copy-start(bf16[384,4096]{1,0:T(8,128)(2,1)S(1)} %fusion.5.refs_5_) | copy-start | bytes 9437188
  491.8 7.5 %copy-start.61 = (f32[384]{0:T(512)S(1)}, f32[384]{0:T(512)}, u32[]{:S(2)}) copy-start(f32[384]{0:T(512)} %copy-done.60) | copy-start | bytes 4612
  491.8 8.6 %copy-start.52 = (f32[384]{0:T(512)S(1)}, f32[384]{0:T(512)}, u32[]{:S(2)}) copy-start(f32[384]{0:T(512)} %copy-done.51) | copy-start | bytes 4612
  499.2 1.9 copy-start.64
  499.2 1.9 copy-start.65
  499.3 1.9 copy-start.66
  499.3 1.9 copy-start.67
  499.3 1.9 copy-start.68
  691.7 4.3 copy-start.37
  695.9 2.5 copy-start.36
  698.4 2.5 copy-start.35
  700.9 2.5 copy-start.34
  703.4 2.5 copy-start.38
  705.9 1.6 copy-start.42
  705.9 2.7 copy-start.41
  707.5 2.2 copy-start.55
  707.5 4.0 copy-start.16
  707.5 4.0 copy-start.17
  (19 other events, 22.8 us)
where the time goes:
time: 718 us; the launch traced here: 714 us
  Pallas kernels  540 us (75%)
  matrix products  92 us (13%)
  other arithmetic  50 us (7%)
  local copies, waits for them, and re-layouts  27.6 us (4%)
    pallas_call x2, Pallas kernels, sum_products(): pl.pallas_call(partial(sums_kernel, n, plan, small is not None), out_shap...  265 us
    pallas_call x1, Pallas kernels, gather_all(): pl.pallas_call(partial(gather_kernel, n, count), out_shape=[jax.ShapeDtyp...  196 us
    pallas_call x1, Pallas kernels, spread_all(): pl.pallas_call(partial(spread_kernel, count), out_shape=[jax.ShapeDtypeSt...  57.5 us
    dot_general x8, matrix products, right_product(): lax.dot_general(left_side, right_side, (((1,), (1,)), ((), ())), preferre...  51.9 us
    dot_general x10, matrix products, matmul(): return jnp.dot(left_side, right_side, preferred_element_type=jnp.float32)  40.1 us
    unnamed x182, local copies, waits for them, and re-layouts  18.3 us
    convert_element_type x8, other arithmetic, on_device(): grads = [s.astype(jnp.float32) for s in sums]  17.9 us

commit v1 on v0

--- a/solution.py
+++ b/solution.py
@@ -310,6 +310,10 @@
     return pl.ds(pl.multiple_of(start, 16), count)
 
 
+ORDER = (0, 1, 2, 4, 6, 7, 3, 5)
+DIRECT = (3, 5)
+
+
 def gather_kernel(n, count, *refs):
     shards = refs[: count + 1]
     fulls = refs[count + 1 : 2 * count + 2]
@@ -318,8 +322,8 @@
     d = lax.axis_index("dp")
     core, place = d % 2, d // 2
     x_peer, y_peer, core_peer = {"dp": flip_x(d)}, {"dp": flip_y(d)}, {"dp": other_core(d)}
-    z_peers = [{"fsdp": (z + k) % n} for k in range(1, n)]
-    greet(z_peers + [x_peer, y_peer, core_peer])
+    up, down = {"fsdp": (z + 1) % n}, {"fsdp": (z + n - 1) % n}
+    greet([up, down, x_peer, y_peer, core_peer])
     used = [0]
     started = []
 
@@ -338,26 +342,27 @@
         started.append(copy)
         return copy
 
+    flip_1 = place + 1 - 2 * (place % 2)
+    flip_2 = place + 2 - 4 * (place // 2)
+
+    def span(t, owner):
+        depth = shards[t].shape[0]
+        if t == count:
+            return rows_of(owner * depth, depth)
+        if t in DIRECT:
+            return rows_of(owner * depth + core * (depth // 2), depth // 2)
+        return rows_of(owner * depth + (core * 4 + place) * (depth // 8), depth // 8)
+
     first = {}
-    for t in range(count):
-        depth = shards[t].shape[0]
-        part = depth // 8
-        for k in range(1, n):
-            first[t, k] = send(
-                shards[t].at[rows_of((core * 4 + place) * part, part), :],
-                fulls[t].at[rows_of(z * depth + (core * 4 + place) * part, part), :],
-                z_peers[k - 1],
-            )
-    late = []
-    small = shards[count].shape[0]
-    for k in range(1, n):
-        late.append(send(shards[count], fulls[count].at[rows_of(z * small, small), :], z_peers[k - 1]))
-    for t in range(count + 1):
-        depth = shards[t].shape[0]
-        late.append(send(shards[t], fulls[t].at[rows_of(z * depth, depth), :], core_peer))
-
-    stages = [(t, k) for t in range(count) for k in range(1, n)]
-    across, corner = {}, {}
+
+    def launch(t):
+        view = shards[t].at[span(t, 0), :]
+        first[t, 1] = send(view, fulls[t].at[span(t, z), :], up)
+        first[t, 3] = send(view, fulls[t].at[span(t, z), :], down)
+
+    def relay(t):
+        view = fulls[t].at[span(t, (z + n - 1) % n), :]
+        first[t, 2] = send(view, view, up)
 
     def piece(t, k, where, half=None):
         depth = shards[t].shape[0]
@@ -367,12 +372,31 @@
             return fulls[t].at[rows_of(start, part), :]
         return fulls[t].at[rows_of(start + half * (part // 2), part // 2), :]
 
-    flip_1 = place + 1 - 2 * (place % 2)
-    flip_2 = place + 2 - 4 * (place // 2)
+    late = []
+
+    def to_core(t, k):
+        depth = shards[t].shape[0]
+        half = depth // 2
+        view = fulls[t].at[rows_of(((z + n - k) % n) * depth + core * half, half), :]
+        late.append(send(view, view, core_peer))
+
+    launch(ORDER[0])
+    launch(count)
+    launch(ORDER[1])
+    for t in [*ORDER, count]:
+        depth = shards[t].shape[0]
+        late.append(send(shards[t], fulls[t].at[rows_of(z * depth, depth), :], core_peer))
+    stages = [(t, k) for t in ORDER if t not in DIRECT for k in (1, 3, 2)]
+    across, corner = {}, {}
     for i in range(len(stages) + 2):
         if i < len(stages):
             t, k = stages[i]
             first[t, k].wait_recv()
+            if k == 1:
+                relay(t)
+                following = ORDER.index(t) + 2
+                if following < count:
+                    launch(ORDER[following])
             mine = piece(t, k, place)
             across[i] = (send(mine, mine, x_peer), send(mine, mine, y_peer))
         if 0 <= i - 1 < len(stages):
@@ -385,13 +409,19 @@
             view = piece(t, k, flip_1, 1)
             corner[i - 1] = (one, send(view, view, y_peer))
         if 0 <= i - 2 < len(stages):
-            t, k = stages[i - 2]
             for copy in corner[i - 2]:
                 copy.wait_recv()
-            depth = shards[t].shape[0]
-            half = depth // 2
-            view = fulls[t].at[rows_of(((z + n - k) % n) * depth + core * half, half), :]
-            late.append(send(view, view, core_peer))
+            to_core(*stages[i - 2])
+    for t in [*DIRECT, count]:
+        first[t, 1].wait_recv()
+        relay(t)
+    for k in (1, 3, 2):
+        for t in DIRECT:
+            if k > 1:
+                first[t, k].wait_recv()
+            to_core(t, k)
+    for k in (2, 3):
+        first[count, k].wait_recv()
     for copy in late:
         copy.wait_recv()
     for copy in started:
@@ -401,7 +431,7 @@
 def gather_all(n, shards, small, collective_id):
     count = len(shards)
     given = list(shards) + [small]
-    copies = count * (n - 1) * 6 + (n - 1) + count + 1
+    copies = count * (n - 1) * 6 + n + count
     return pl.pallas_call(
         partial(gather_kernel, n, count),
         out_shape=[jax.ShapeDtypeStruct((n * s.shape[0], s.shape[1]), s.dtype) for s in given],
@@ -735,8 +765,8 @@
     )(*operands)
 
 
-EARLY = (6, 7, 4, 5, 3)
-LATE = (2, 0, 1)
+EARLY = (6, 7, 4, 5)
+LATE = (2, 0, 1, 3)
 
 
 def fallback_reduce(pairs):

time: 718 us -> 689 us (0.960)
  Pallas kernels: 540 us -> 514 us
    pallas_call x1, Pallas kernels: 196 us -> 177 us  [gather_all(): pl.pallas_call(partial(gather_kernel, n, count), out_shape=[jax.ShapeDtyp...]
    unnamed x182 -> x164, local copies, waits for them, and re-layouts: 18.3 us -> 14 us
where the time goes in v1:
time: 689 us; the launch traced here: 685 us
  Pallas kernels  514 us (75%)
  matrix products  89.7 us (13%)
  other arithmetic  50.6 us (7%)
  local copies, waits for them, and re-layouts  27 us (4%)
    pallas_call x2, Pallas kernels, sum_products(): pl.pallas_call(partial(sums_kernel, n, plan, small is not None), out_shap...  258 us
    pallas_call x1, Pallas kernels, gather_all(): pl.pallas_call(partial(gather_kernel, n, count), out_shape=[jax.ShapeDtyp...  177 us
    pallas_call x1, Pallas kernels, spread_all(): pl.pallas_call(partial(spread_kernel, count), out_shape=[jax.ShapeDtypeSt...  57 us
    dot_general x8, matrix products, right_product(): lax.dot_general(left_side, right_side, (((1,), (1,)), ((), ())), preferre...  49.6 us
    dot_general x10, matrix products, matmul(): return jnp.dot(left_side, right_side, preferred_element_type=jnp.float32)  40 us
    convert_element_type x8, other arithmetic, on_device(): grads = [s.astype(jnp.float32) for s in sums]  17.9 us
    unnamed x164, local copies, waits for them, and re-layouts  14 us

profile of v1, /device:TPU:0, one launch (start us, length us, event | category | flops | bytes accessed | tf_op | source)
XLA Modules:
  0.0 684.9 jit_solution(12772933713550701623)
XLA Ops:
  0.7 1.4 maximum_maximum_fusion.refs_8_
  2.1 177.0 %gather_weights.1 = (bf16[1024,4096]{1,0:T(8,128)(2,1)}, bf16[4096,1024]{1,0:T(8,128)(2,1)}, bf16[1024,4096]{1,0:T(8,128)(2,1)}, bf16[1024,1024]{1,0:T(8,128)(2,...) custom-call(bf16[256,4096]{1,0:T(8,128)(2,1)} %refs_0_.1, ...), custom_call_target="tpu_custom_call" | custom-call | tf_op jit(solution)/shard_map/gather_weights/pallas_call | solution.py:435
  179.1 0.8 copy.43
  181.7 9.9 %multiply_convert_fusion.1 = (bf16[384,4096]{1,0:T(8,128)(2,1)S(1)}, f32[384,4096]{1,0:T(8,128)}) fusion(bf16[384,1024]{1,0:T(8,128)(2,1)S(1)} %fusion.25.refs_4_, bf16[1024,4096]{1,0:T(8,128)(2,1)} %get-tuple-element.55), kind=kOutput, calls=%fused_computation.10 | convolution fusion | flops 3229089792 | bytes 18612224 | tf_op jit(solution)/shard_map/dot_general | solution.py:24
  191.6 3.6 fusion.103
  195.8 3.9 fusion.10.q_ref.k_ref.v_ref
  202.5 0.8 add_convert_fusion.3.allow_ref
  203.8 0.8 multiply_cosine_fusion
  204.8 3.5 fusion.41.pos_ref
  208.9 10.2 %attend.1 = (bf16[384,1024]{1,0:T(8,128)(2,1)}, bf16[2,8,192,192]{3,2,1,0:T(8,128)(2,1)}) custom-call(bf16[384,3072]{1,0:T(8,128)(2,1)} %fusion.10.q_ref.k_ref.v_ref, bf16[384,3072]{1,0:T(8,128)(2,1)} %fusion.10.q_ref.k_ref.v_ref, bf16[384,3072]{1,0:T(8,128)(2,1)} %fusion.10.q_ref.k_ref.v_ref, f32[2,1024]{1,0:T(2,128)} %bitcast.105, ...), custom_call_target="tpu_custom_call" | custom-call | tf_op jit(solution)/shard_map/attend/pallas_call | solution.py:197
  219.1 3.0 fusion.104
  223.3 1.8 fusion.107
  225.6 1.9 fusion.92
  227.5 1.9 fusion.93
  229.7 0.7 fusion.67
  232.0 0.7 stack.38
  233.0 0.7 fusion.68
  235.2 0.8 stack.41
  236.2 4.6 fusion.91
  241.7 0.7 copy-done.62
  242.4 0.8 copy-done.5
  243.2 1.1 fusion.105
  244.9 6.3 multiply_convert_fusion
  251.3 3.6 fusion.106
  255.2 0.8 copy-done.30
  256.0 0.6 fusion.28
  256.6 1.5 fusion.90
  258.4 11.1 %fusion.2.refs_1_ = bf16[384,4096]{1,0:T(8,128)(2,1)S(1)} fusion(f32[384,4096]{1,0:T(8,128)} %get-tuple-element.198, bf16[384,1024]{1,0:T(8,128)(2,1)S(1)} %multiply_convert_fusion.3.refs_3_, bf16[4096,1024]{1,0:T(8,128)(2,1)} %get-tuple-element.67), kind=kOutput, calls=%fused_computation.4 | convolution fusion | flops 3236954112 | bytes 18612224 | tf_op jit(solution)/shard_map/dot_general | solution.py:34
  269.5 7.9 %multiply_reduce_fusion.5 = (f32[1024]{0:T(1024)}, f32[384]{0:T(512)S(1)}, f32[384,1024]{1,0:T(8,128)S(1)}) fusion(f32[384,1024]{1,0:T(8,128)S(1)} %get-tuple-element.196, f32[384]{0:T(512)S(1)} %fusion.75, f32[384]{0:T(512)S(1)} %broadcast_multiply_fusion.1, f32[1024]{0:T(1024)S(1)} %bitcast.131, bf16[384,4096]{1,0:T(8,128)(2,1)S(1)} %fusion.2.refs_1_, ...), kind=kOutput, calls=%fused_computation.69 | convolution fusion | flops 3223976448 | bytes 14692864 | tf_op jit(solution)/shard_map/dot_general | solution.py:34
  277.9 1.4 fusion.88
  279.4 0.7 copy-done.63
  280.1 2.3 multiply_reduce_fusion.6
  283.0 0.8 copy-done.8
  284.7 2.7 multiply_reduce_fusion.4
  288.3 1.4 fusion.33
  290.2 1.4 add_convert_fusion.refs_5_
  291.6 117.8 %sum_products.3 = (bf16[32,4096]{1,0:T(8,128)(2,1)}, bf16[128,1024]{1,0:T(8,128)(2,1)}, bf16[32,2048]{1,0:T(8,128)(2,1)}, bf16[32,1024]{1,0:T(8,128)(2,1)}) custom-call(bf16[384,1024]{1,0:T(8,128)(2,1)} %copy-done.25, bf16[384,4096]{1,0:T(8,128)(2,1)} %copy-done.29, bf16[384,4096]{1,0:T(8,128)(2,1)} %copy-done.28, bf16[384,1024]{1,0:T(8,128)(2,1)} %copy-done.26, ...), custom_call_target="tpu_custom_call" | custom-call | tf_op jit(solution)/shard_map/sum_products/pallas_call | solution.py:751
  409.4 5.4 multiply_reduce_fusion.7
  415.4 0.9 copy-done.7
  416.4 1.4 copy-done.61
  417.8 1.9 convolution_convert_fusion.grad_ref
  419.9 0.9 copy-done.27
  420.8 3.5 fusion.44.pos_ref
  424.3 12.2 %attend_back.1 = (bf16[384,1024]{1,0:T(8,128)(2,1)}, bf16[384,1024]{1,0:T(8,128)(2,1)}, bf16[384,1024]{1,0:T(8,128)(2,1)}, bf16[384,1024]{1,0:T(8,128)(2,1)}, f32[2,1024]{1,0:T(2,128)}) custom-call(bf16[384,3072]{1,0:T(8,128)(2,1)} %fusion.10.q_ref.k_ref.v_ref, bf16[384,3072]{1,0:T(8,128)(2,1)} %fusion.10.q_ref.k_ref.v_ref, ...), custom_call_target="tpu_custom_call" | custom-call | tf_op jit(solution)/shard_map/attend_back/pallas_call | solution.py:220
  436.5 1.3 constant_dynamic-update-slice_fusion.2
  438.1 1.2 copy-done.3
  439.3 5.9 multiply_reduce_fusion.8
  445.8 1.5 multiply_convert_fusion.2
  447.4 11.6 %fusion.5.refs_5_ = bf16[384,4096]{1,0:T(8,128)(2,1)S(1)} fusion(f32[384,4096]{1,0:T(8,128)} %get-tuple-element.190, bf16[384,1024]{1,0:T(8,128)(2,1)S(1)} %get-tuple-element.118.refs_7_, bf16[4096,1024]{1,0:T(8,128)(2,1)} %get-tuple-element.56), kind=kOutput, calls=%fused_computation.7 | convolution fusion | flops 3236954112 | bytes 18612224 | tf_op jit(solution)/shard_map/dot_general | solution.py:34
  459.2 3.5 fusion.30
  462.8 1.1 copy-done.12
  463.9 0.8 fusion.26
  464.7 1.3 concatenate.179.refs_10_
  466.0 139.9 %sum_products.2 = (bf16[32,4096]{1,0:T(8,128)(2,1)}, bf16[32,4096]{1,0:T(8,128)(2,1)}, bf16[128,1024]{1,0:T(8,128)(2,1)}, bf16[32,1024]{1,0:T(8,128)(2,1)}, f32[16,256]{1,0:T(8,128)}) custom-call(bf16[384,1024]{1,0:T(8,128)(2,1)} %copy-done.22, bf16[384,3072]{1,0:T(8,128)(2,1)} %copy-done.15, bf16[384,1024]{1,0:T(8,128)(2,1)} %bitcast.101, ...), custom_call_target="tpu_custom_call" | custom-call | tf_op jit(solution)/shard_map/sum_products/pallas_call | solution.py:751
  605.9 57.0 %spread_sums.1 = (bf16[256,4096]{1,0:T(8,128)(2,1)}, bf16[1024,1024]{1,0:T(8,128)(2,1)}, bf16[256,4096]{1,0:T(8,128)(2,1)}, bf16[256,1024]{1,0:T(8,128)(2,1)}, b...) custom-call(bf16[32,4096]{1,0:T(8,128)(2,1)} %get-tuple-element.78.r, ...), custom_call_target="tpu_custom_call" | custom-call | tf_op jit(solution)/shard_map/spread_sums/pallas_call | solution.py:518
  663.0 4.2 convert_element_type.266
  667.2 2.5 convert_element_type.267
  669.7 2.5 convert_element_type.268
  672.2 2.5 convert_element_type.272
  674.7 2.5 convert_element_type.273
  677.2 1.6 convert_element_type.270
  678.8 1.1 convert_element_type.269
  679.9 1.1 convert_element_type.271
  682.7 1.7 add_add_fusion.6
  (254 shorter events, 19.7 us)
Async XLA Ops:
  2.1 177.8 %copy-start = (bf16[384,1024]{1,0:T(8,128)(2,1)S(1)}, bf16[384,1024]{1,0:T(8,128)(2,1)}, u32[]{:S(2)}) copy-start(bf16[384,1024]{1,0:T(8,128)(2,1)} %param.15) | copy-start | bytes 2359300
  179.9 1.5 copy-start.40
  181.1 10.4 %slice-start.2 = ((s8[8388608]{0:T(1024)(128)(4,1)}), s8[4194304]{0:T(1024)(128)(4,1)S(1)}, s32[]{:S(2)}) async-start(s8[8388608]{0:T(1024)(128)(4,1)} %bitcast.157), calls=%async_computation.2 | async-start | bytes 8388608
  181.1 14.7 %slice-start.4 = ((s8[8388608]{0:T(1024)(128)(4,1)}), s8[4194304]{0:T(1024)(128)(4,1)S(1)}, s32[]{:S(2)}) async-start(s8[8388608]{0:T(1024)(128)(4,1)} %bitcast.159), calls=%async_computation.4 | async-start | bytes 8388608
  181.7 9.9 %copy-start.21 = (bf16[384,1024]{1,0:T(8,128)(2,1)}, bf16[384,1024]{1,0:T(8,128)(2,1)S(1)}, u32[]{:S(2)}) copy-start(bf16[384,1024]{1,0:T(8,128)(2,1)S(1)} %fusion.25.refs_4_) | copy-start | bytes 2359300
  181.7 9.9 %slice-start.3 = ((s8[8388608]{0:T(1024)(128)(4,1)}), s8[4194304]{0:T(1024)(128)(4,1)S(1)}, s32[]{:S(2)}) async-start(s8[8388608]{0:T(1024)(128)(4,1)} %bitcast.157), calls=%async_computation.3 | async-start | bytes 8388608
  181.7 14.1 %slice-start.5 = ((s8[8388608]{0:T(1024)(128)(4,1)}), s8[4194304]{0:T(1024)(128)(4,1)S(1)}, s32[]{:S(2)}) async-start(s8[8388608]{0:T(1024)(128)(4,1)} %bitcast.159), calls=%async_computation.5 | async-start | bytes 8388608
  191.6 3.6 copy-start.16
  195.1 24.0 %copy-start.2 = (f32[384,1024]{1,0:T(8,128)}, f32[384,1024]{1,0:T(8,128)S(1)}, u32[]{:S(2)}) copy-start(f32[384,1024]{1,0:T(8,128)S(1)} %get-tuple-element.192) | copy-start | bytes 4718596
  195.8 3.9 copy-start.22
  195.8 3.9 copy-start.58
  195.8 5.2 copy-start.59
  202.2 6.1 copy-start.53
  219.1 4.2 copy-start.60
  223.3 1.8 copy-start.23
  227.5 4.3 copy-start.54
  227.5 7.6 %copy-start.52 = (s32[192]{0:T(256)S(1)}, s32[192]{0:T(256)}, u32[]{:S(2)}) copy-start(s32[192]{0:T(256)} %copy-done.51) | copy-start | bytes 2308
  236.2 8.7 %slice-start.6 = ((s8[8388608]{0:T(1024)(128)(4,1)}), s8[4194304]{0:T(1024)(128)(4,1)S(1)}, s32[]{:S(2)}) async-start(s8[8388608]{0:T(1024)(128)(4,1)} %bitcast.161), calls=%async_computation.6 | async-start | bytes 8388608
  240.8 1.6 copy-start.62
  241.1 2.1 copy-start.5
  241.1 3.8 slice-start.7
  241.7 2.5 copy-start.24
  244.2 7.0 %slice-start.8 = ((s8[8388608]{0:T(1024)(128)(4,1)}), s8[4194304]{0:T(1024)(128)(4,1)S(1)}, s32[]{:S(2)}) async-start(s8[8388608]{0:T(1024)(128)(4,1)} %bitcast.163), calls=%async_computation.8 | async-start | bytes 8388608
  244.9 6.4 copy-start.25
  244.9 6.4 slice-start.9
  251.2 3.6 copy-start.28
  258.4 11.1 %copy-start.26 = (bf16[384,1024]{1,0:T(8,128)(2,1)}, bf16[384,1024]{1,0:T(8,128)(2,1)S(1)}, u32[]{:S(2)}) copy-start(bf16[384,1024]{1,0:T(8,128)(2,1)S(1)} %multiply_convert_fusion.3.refs_3_) | copy-start | bytes 2359300
  269.5 7.9 %copy-start.29 = (bf16[384,4096]{1,0:T(8,128)(2,1)}, bf16[384,4096]{1,0:T(8,128)(2,1)S(1)}, u32[]{:S(2)}) copy-start(bf16[384,4096]{1,0:T(8,128)(2,1)S(1)} %fusion.2.refs_1_) | copy-start | bytes 9437188
  277.9 2.2 copy-start.63
  279.4 3.0 copy-start.19
  280.1 2.8 copy-start.11
  282.4 1.4 copy-start.8
  282.4 1.9 copy-start.9
  282.4 2.3 copy-start.10
  291.6 117.8 %copy-start.49 = (f32[1024]{0:T(1024)S(1)}, f32[1024]{0:T(1024)}, u32[]{:S(2)}) copy-start(f32[1024]{0:T(1024)} %get-tuple-element.110) | copy-start | bytes 12292
  291.6 117.8 %copy-start.50 = (f32[1024]{0:T(1024)S(1)}, f32[1024]{0:T(1024)}, u32[]{:S(2)}) copy-start(f32[1024]{0:T(1024)} %get-tuple-element.111) | copy-start | bytes 12292
  409.4 5.4 copy-start.6
  416.2 1.6 copy-start.61
  417.8 1.9 copy-start.18
  436.5 1.6 copy-start.36
  437.9 1.5 copy-start.3
  439.3 5.9 copy-start.15
  445.8 13.2 %slice-start = ((s8[8388608]{0:T(1024)(128)(4,1)}), s8[4194304]{0:T(1024)(128)(4,1)S(1)}, s32[]{:S(2)}) async-start(s8[8388608]{0:T(1024)(128)(4,1)} %bitcast.155), calls=%async_computation | async-start | bytes 8388608
  447.4 11.7 %copy-start.20 = (bf16[384,1024]{1,0:T(8,128)(2,1)}, bf16[384,1024]{1,0:T(8,128)(2,1)S(1)}, u32[]{:S(2)}) copy-start(bf16[384,1024]{1,0:T(8,128)(2,1)S(1)} %get-tuple-element.118.refs_7_) | copy-start | bytes 2359300
  447.4 11.7 %copy-start.1 = (bf16[384,1024]{1,0:T(8,128)(2,1)S(1)}, bf16[384,1024]{1,0:T(8,128)(2,1)}, u32[]{:S(2)}) copy-start(bf16[384,1024]{1,0:T(8,128)(2,1)} %param.15) | copy-start | bytes 2359300
  447.4 11.7 %copy-start.41 = (f32[1,2,4,128]{3,1,2,0:T(2,128)S(1)}, f32[1,2,4,128]{3,1,2,0:T(2,128)}, u32[]{:S(2)}) copy-start(f32[1,2,4,128]{3,1,2,0:T(2,128)} %copy-done.40) | copy-start | bytes 12292
  447.4 11.7 %copy-start.43 = (f32[384]{0:T(512)S(1)}, f32[384]{0:T(512)}, u32[]{:S(2)}) copy-start(f32[384]{0:T(512)} %copy-done.42) | copy-start | bytes 4612
  447.4 11.7 %slice-start.1 = ((s8[8388608]{0:T(1024)(128)(4,1)}), s8[4194304]{0:T(1024)(128)(4,1)S(1)}, s32[]{:S(2)}) async-start(s8[8388608]{0:T(1024)(128)(4,1)} %bitcast.155), calls=%async_computation.1 | async-start | bytes 8388608
  459.1 3.6 copy-start.17
  459.1 3.6 copy-start.48
  459.2 4.7 copy-start.45
  462.7 1.9 copy-start.55
  462.7 1.9 copy-start.56
  462.8 1.9 copy-start.57
  663.0 4.3 copy-start.34
  667.2 2.5 copy-start.33
  669.7 2.5 copy-start.32
  672.2 2.5 copy-start.31
  674.7 2.5 copy-start.35
  677.2 1.6 copy-start.39
  677.2 2.7 copy-start.38
  678.8 2.2 copy-start.46
  678.8 4.0 copy-start.13
  678.8 4.0 copy-start.14
  (10 other events, 10.5 us)

commit v2 on v1

--- a/solution.py
+++ b/solution.py
@@ -443,93 +443,6 @@
     )(*given)
 
 
-def spread_kernel(count, *refs):
-    pieces = refs[:count]
-    wholes = refs[count : 2 * count]
-    send_sem, recv_sem, own_sem = refs[2 * count :]
-    d = lax.axis_index("dp")
-    core, place = d % 2, d // 2
-    x_peer, y_peer, core_peer = {"dp": flip_x(d)}, {"dp": flip_y(d)}, {"dp": other_core(d)}
-    greet([x_peer, y_peer, core_peer])
-    used = [0]
-    started = []
-
-    def send(src, dst, peer):
-        index = used[0]
-        used[0] += 1
-        copy = pltpu.make_async_remote_copy(
-            src_ref=src,
-            dst_ref=dst,
-            send_sem=send_sem.at[index],
-            recv_sem=recv_sem.at[index],
-            device_id=peer,
-            device_id_type=MESH,
-        )
-        copy.start()
-        started.append(copy)
-        return copy
-
-    flip_1 = place + 1 - 2 * (place % 2)
-    flip_2 = place + 2 - 4 * (place // 2)
-
-    def region(t, owner_core, where, half=None):
-        part = pieces[t].shape[0]
-        start = (owner_core * 4 + where) * part
-        if half is None:
-            return wholes[t].at[rows_of(start, part), :]
-        return wholes[t].at[rows_of(start + half * (part // 2), part // 2), :]
-
-    across, own, late = [], [], []
-    for t in range(count):
-        spot = region(t, core, place)
-        across.append((send(pieces[t], spot, x_peer), send(pieces[t], spot, y_peer)))
-        late.append(send(pieces[t], spot, core_peer))
-        keep = pltpu.make_async_copy(pieces[t], spot, own_sem.at[t])
-        keep.start()
-        own.append(keep)
-    corner = []
-    for t in range(count):
-        by_x, by_y = across[t]
-        by_y.wait_recv()
-        view = region(t, core, flip_2, 0)
-        one = send(view, view, x_peer)
-        view = region(t, core, flip_2)
-        late.append(send(view, view, core_peer))
-        by_x.wait_recv()
-        view = region(t, core, flip_1, 1)
-        corner.append((one, send(view, view, y_peer)))
-        view = region(t, core, flip_1)
-        late.append(send(view, view, core_peer))
-    for t in range(count):
-        for copy in corner[t]:
-            copy.wait_recv()
-        view = region(t, core, 3 - place)
-        late.append(send(view, view, core_peer))
-    for copy in own:
-        copy.wait()
-    for copy in late:
-        copy.wait_recv()
-    for copy in started:
-        copy.wait_send()
-
-
-def spread_all(pieces, collective_id):
-    count = len(pieces)
-    return pl.pallas_call(
-        partial(spread_kernel, count),
-        out_shape=[jax.ShapeDtypeStruct((8 * s.shape[0], s.shape[1]), s.dtype) for s in pieces],
-        in_specs=[pl.BlockSpec(memory_space=pltpu.VMEM)] * count,
-        out_specs=[pl.BlockSpec(memory_space=pltpu.HBM)] * count,
-        scratch_shapes=[
-            pltpu.SemaphoreType.DMA((8 * count,)),
-            pltpu.SemaphoreType.DMA((8 * count,)),
-            pltpu.SemaphoreType.DMA((count,)),
-        ],
-        compiler_params=pltpu.CompilerParams(collective_id=collective_id, has_side_effects=True),
-        name="spread_sums",
-    )(*pieces)
-
-
 def add_rows(dst, dst_row, src, src_row, count):
     @pl.loop(0, count // 16)
     def _(step):
@@ -539,23 +452,28 @@
         dst[at, :] = total.astype(jnp.bfloat16)
 
 
-def sums_kernel(n, plan, small, *refs):
+def sums_kernel(n, plan, extra, *refs):
+    small = extra > 0
     count = len(plan)
     inputs = sum(2 * len(widths) for _, widths in plan)
     operands = list(refs[:inputs])
     refs = refs[inputs:]
     if small:
         small_ref, refs = refs[0], refs[1:]
-    outs, refs = refs[:count], refs[count:]
-    if small:
+        ready, refs = list(refs[:extra]), refs[extra:]
+        wholes, refs = refs[: extra + count], refs[extra + count :]
         small_out, refs = refs[0], refs[1:]
+        outs, refs = refs[:count], refs[count:]
+    else:
+        outs, refs = refs[:count], refs[count:]
     held, refs = refs[:count], refs[count:]
     from_core, refs = refs[:count], refs[count:]
     from_first, refs = refs[:count], refs[count:]
     from_second, refs = refs[:count], refs[count:]
     from_z, refs = refs[:count], refs[count:]
     if small:
-        (small_held, small_got, small_z), refs = refs[:3], refs[3:]
+        (small_held, small_got, small_z, own_sem), refs = refs[:4], refs[4:]
+        ready += list(outs)
     send_sem, recv_sem = refs
     pairs = []
     for _, widths in plan:
@@ -586,6 +504,56 @@
         if keep:
             started.append(copy)
         return copy
+
+    flip_1 = place + 1 - 2 * (place % 2)
+    flip_2 = place + 2 - 4 * (place // 2)
+    across, corner, own, late = {}, {}, [], []
+
+    def region(t, where, half=None):
+        rows = ready[t].shape[0]
+        start = (core * 4 + where) * rows
+        if half is None:
+            return wholes[t].at[rows_of(start, rows), :]
+        return wholes[t].at[rows_of(start + half * (rows // 2), rows // 2), :]
+
+    def spread_open(t):
+        spot = region(t, place)
+        across[t] = (send(ready[t], spot, peers[0]), send(ready[t], spot, peers[1]))
+        late.append(send(ready[t], spot, core_peer))
+        own.append(pltpu.make_async_copy(ready[t], spot, own_sem.at[t]))
+        own[-1].start()
+
+    def spread_turn(t):
+        by_x, by_y = across[t]
+        by_y.wait_recv()
+        view = region(t, flip_2, 0)
+        one = send(view, view, peers[0])
+        view = region(t, flip_2)
+        late.append(send(view, view, core_peer))
+        by_x.wait_recv()
+        view = region(t, flip_1, 1)
+        corner[t] = (one, send(view, view, peers[1]))
+        view = region(t, flip_1)
+        late.append(send(view, view, core_peer))
+
+    def spread_close(t):
+        for copy in corner[t]:
+            copy.wait_recv()
+        view = region(t, 3 - place)
+        late.append(send(view, view, core_peer))
+
+    def finish(t):
+        p = part[t]
+        for k in range(1, n):
+            third[t, k].wait_recv()
+
+        @pl.loop(0, p // 16)
+        def _(step):
+            total = held[t][pl.ds(pl.multiple_of(place * p + step * 16, 16), 16), :].astype(jnp.float32)
+            for k in range(1, n):
+                at = pl.ds(pl.multiple_of((k - 1) * p + step * 16, 16), 16)
+                total = total + from_z[t][at, :].astype(jnp.float32)
+            outs[t][pl.ds(pl.multiple_of(step * 16, 16), 16), :] = total.astype(jnp.bfloat16)
 
     units = [(t, k) for t in range(count) for k in [*range(1, n), 0]]
     part = [rows // (8 * n) for rows, _ in plan]
@@ -693,18 +661,36 @@
                     from_z[t].at[pl.ds((k - 1) * p, p), :],
                     z_peers[k - 1],
                 )
-    for t in range(count):
-        p = part[t]
-        for k in range(1, n):
-            third[t, k].wait_recv()
-
-        @pl.loop(0, p // 16)
-        def _(step):
-            total = held[t][pl.ds(pl.multiple_of(place * p + step * 16, 16), 16), :].astype(jnp.float32)
-            for k in range(1, n):
-                at = pl.ds(pl.multiple_of((k - 1) * p + step * 16, 16), 16)
-                total = total + from_z[t][at, :].astype(jnp.float32)
-            outs[t][pl.ds(pl.multiple_of(step * 16, 16), 16), :] = total.astype(jnp.bfloat16)
+        if small:
+            for t in range(count - 1):
+                if i == n * (t + 1) + 8:
+                    finish(t)
+                    spread_open(extra + t)
+                if i == n * (t + 1) + 11:
+                    spread_turn(extra + t)
+            at = i - (len(units) - extra)
+            if 0 <= at < extra:
+                spread_open(at)
+            if 0 <= at - 2 < extra:
+                spread_turn(at - 2)
+    if small:
+        opened = {t for t in range(count - 1) if n * (t + 1) + 8 < len(units) + 6}
+        for t in range(count):
+            if t not in opened:
+                finish(t)
+                spread_open(extra + t)
+        for t in range(extra + count):
+            if t not in corner:
+                spread_turn(t)
+        for t in range(extra + count):
+            spread_close(t)
+        for copy in own:
+            copy.wait()
+        for copy in late:
+            copy.wait_recv()
+    else:
+        for t in range(count):
+            finish(t)
 
     if small:
         for copy in small_z_copies:
@@ -717,7 +703,7 @@
         copy.wait_send()
 
 
-def sum_products(n, tensors, small, collective_id):
+def sum_products(n, tensors, small, ready, collective_id):
     plan = [
         (pairs[0][0].shape[1], tuple(right.shape[1] for _, right in pairs)) for pairs in tensors
     ]
@@ -737,22 +723,29 @@
         *room(n - 1, 8 * n),
     ]
     copies = count * (5 * n - 1)
+    whole = pl.BlockSpec(memory_space=pltpu.VMEM)
+    out_specs = [whole] * count
     if small is not None:
-        operands.append(small)
+        operands += [small, *ready]
         depth, width = small.shape
-        out_shape.append(jax.ShapeDtypeStruct((depth, width // n), jnp.float32))
-        scratch += [
+        pieces = [pltpu.VMEM(s.shape, jnp.bfloat16) for s in out_shape]
+        out_shape = [
+            *[jax.ShapeDtypeStruct((8 * s.shape[0], s.shape[1]), s.dtype) for s in [*ready, *out_shape]],
+            jax.ShapeDtypeStruct((depth, width // n), jnp.float32),
+        ]
+        out_specs = [pl.BlockSpec(memory_space=pltpu.HBM)] * (len(out_shape) - 1) + [whole]
+        scratch = pieces + scratch + [
             pltpu.VMEM((depth, width), jnp.float32),
             pltpu.VMEM((3, depth, width), jnp.float32),
             pltpu.VMEM((n - 1, depth, width // n), jnp.float32),
+            pltpu.SemaphoreType.DMA((len(ready) + count,)),
         ]
-        copies += 3 + n - 1
-    whole = pl.BlockSpec(memory_space=pltpu.VMEM)
+        copies += 3 + n - 1 + 8 * (len(ready) + count)
     return pl.pallas_call(
-        partial(sums_kernel, n, plan, small is not None),
+        partial(sums_kernel, n, plan, 0 if small is None else len(ready)),
         out_shape=out_shape,
         in_specs=[whole] * len(operands),
-        out_specs=[whole] * len(out_shape),
+        out_specs=out_specs,
         scratch_shapes=[
             *scratch,
             pltpu.SemaphoreType.DMA((copies,)),
@@ -867,11 +860,10 @@
     )
     tensors = [grad_in1, grad_out1, grad_in2, grad_out2, grad_in3, grad_out3, grad_in4, grad_out4]
     if fast:
-        early = sum_products(n, [tensors[i] for i in EARLY], None, 2)
-        *late, grad_small = sum_products(n, [tensors[i] for i in LATE], grad_vectors, 3)
-        for index, total in zip(EARLY + LATE, list(early) + late):
+        early = sum_products(n, [tensors[i] for i in EARLY], None, (), 1)
+        *wholes, grad_small = sum_products(n, [tensors[i] for i in LATE], grad_vectors, early, 2)
+        for index, total in zip(EARLY + LATE, wholes):
             sums[index] = total
-        sums = spread_all(sums, 1)
     else:
         sums = [fallback_reduce(pairs) for pairs in tensors]
         grad_small = lax.psum(

time: 689 us -> 678 us (0.984)
  Pallas kernels: 514 us -> 503 us
    pallas_call x3 -> x2, Pallas kernels: 315 us -> 304 us  [sum_products(): pl.pallas_call(partial(sums_kernel, n, plan, 0 if small is None else len(...]
where the time goes in v2:
time: 678 us; the launch traced here: 674 us
  Pallas kernels  503 us (74%)
  matrix products  89.8 us (13%)
  other arithmetic  50.6 us (7%)
  local copies, waits for them, and re-layouts  27 us (4%)
    pallas_call x2, Pallas kernels, sum_products(): pl.pallas_call(partial(sums_kernel, n, plan, 0 if small is None else len(...  304 us
    pallas_call x1, Pallas kernels, gather_all(): pl.pallas_call(partial(gather_kernel, n, count), out_shape=[jax.ShapeDtyp...  177 us
    dot_general x8, matrix products, right_product(): lax.dot_general(left_side, right_side, (((1,), (1,)), ((), ())), preferre...  49.6 us
    dot_general x10, matrix products, matmul(): return jnp.dot(left_side, right_side, preferred_element_type=jnp.float32)  40.1 us
    convert_element_type x8, other arithmetic, on_device(): grads = [s.astype(jnp.float32) for s in sums]  17.9 us
    unnamed x164, local copies, waits for them, and re-layouts  14 us

profile of v2, /device:TPU:0, one launch (start us, length us, event | category | flops | bytes accessed | tf_op | source)
XLA Modules:
  0.0 674.4 jit_solution(6976922912428808810)
XLA Ops:
  0.7 1.4 maximum_maximum_fusion.refs_8_
  2.1 177.0 %gather_weights.1 = (bf16[1024,4096]{1,0:T(8,128)(2,1)}, bf16[4096,1024]{1,0:T(8,128)(2,1)}, bf16[1024,4096]{1,0:T(8,128)(2,1)}, bf16[1024,1024]{1,0:T(8,128)(2,...) custom-call(bf16[256,4096]{1,0:T(8,128)(2,1)} %refs_0_.1, ...), custom_call_target="tpu_custom_call" | custom-call | tf_op jit(solution)/shard_map/gather_weights/pallas_call | solution.py:435
  179.1 0.8 copy.43
  181.7 9.9 %multiply_convert_fusion.1 = (bf16[384,4096]{1,0:T(8,128)(2,1)S(1)}, f32[384,4096]{1,0:T(8,128)}) fusion(bf16[384,1024]{1,0:T(8,128)(2,1)S(1)} %fusion.25.refs_4_, bf16[1024,4096]{1,0:T(8,128)(2,1)} %get-tuple-element.51), kind=kOutput, calls=%fused_computation.10 | convolution fusion | flops 3229089792 | bytes 18612224 | tf_op jit(solution)/shard_map/dot_general | solution.py:24
  191.6 3.6 fusion.103
  195.8 3.9 fusion.10.q_ref.k_ref.v_ref
  202.4 0.8 add_convert_fusion.3.allow_ref
  203.8 0.8 multiply_cosine_fusion
  204.8 3.5 fusion.41.pos_ref
  208.3 0.6 copy.32
  208.9 10.2 %attend.1 = (bf16[384,1024]{1,0:T(8,128)(2,1)}, bf16[2,8,192,192]{3,2,1,0:T(8,128)(2,1)}) custom-call(bf16[384,3072]{1,0:T(8,128)(2,1)} %fusion.10.q_ref.k_ref.v_ref, bf16[384,3072]{1,0:T(8,128)(2,1)} %fusion.10.q_ref.k_ref.v_ref, bf16[384,3072]{1,0:T(8,128)(2,1)} %fusion.10.q_ref.k_ref.v_ref, f32[2,1024]{1,0:T(2,128)} %bitcast.105, ...), custom_call_target="tpu_custom_call" | custom-call | tf_op jit(solution)/shard_map/attend/pallas_call | solution.py:197
  219.1 3.0 fusion.104
  223.3 1.8 fusion.107
  225.6 1.9 fusion.92
  227.5 1.9 fusion.93
  229.7 0.7 fusion.67
  232.0 0.8 stack.38
  233.0 0.7 fusion.68
  235.3 0.8 stack.41
  236.2 4.6 fusion.91
  241.7 0.7 copy-done.62
  242.4 0.8 copy-done.5
  243.2 1.1 fusion.105
  244.9 6.4 multiply_convert_fusion
  251.4 3.6 fusion.106
  255.3 0.8 copy-done.30
  256.1 0.6 fusion.28
  256.8 1.5 fusion.90
  258.5 11.1 %fusion.2.refs_1_ = bf16[384,4096]{1,0:T(8,128)(2,1)S(1)} fusion(f32[384,4096]{1,0:T(8,128)} %get-tuple-element.190, bf16[384,1024]{1,0:T(8,128)(2,1)S(1)} %multiply_convert_fusion.3.refs_3_, bf16[4096,1024]{1,0:T(8,128)(2,1)} %get-tuple-element.63), kind=kOutput, calls=%fused_computation.4 | convolution fusion | flops 3236954112 | bytes 18612224 | tf_op jit(solution)/shard_map/dot_general | solution.py:34
  269.6 7.9 %multiply_reduce_fusion.5 = (f32[1024]{0:T(1024)}, f32[384]{0:T(512)S(1)}, f32[384,1024]{1,0:T(8,128)S(1)}) fusion(f32[384,1024]{1,0:T(8,128)S(1)} %get-tuple-element.188, f32[384]{0:T(512)S(1)} %fusion.75, f32[384]{0:T(512)S(1)} %broadcast_multiply_fusion.1, f32[1024]{0:T(1024)S(1)} %bitcast.131, bf16[384,4096]{1,0:T(8,128)(2,1)S(1)} %fusion.2.refs_1_, ...), kind=kOutput, calls=%fused_computation.69 | convolution fusion | flops 3223976448 | bytes 14692864 | tf_op jit(solution)/shard_map/dot_general | solution.py:34
  278.1 1.4 fusion.88
  279.5 0.7 copy-done.63
  280.2 2.3 multiply_reduce_fusion.6
  283.1 0.8 copy-done.8
  284.9 2.7 multiply_reduce_fusion.4
  288.5 1.4 fusion.33
  290.3 1.4 add_convert_fusion.refs_5_
  291.7 117.9 %sum_products.2 = (bf16[32,4096]{1,0:T(8,128)(2,1)}, bf16[128,1024]{1,0:T(8,128)(2,1)}, bf16[32,2048]{1,0:T(8,128)(2,1)}, bf16[32,1024]{1,0:T(8,128)(2,1)}) custom-call(bf16[384,1024]{1,0:T(8,128)(2,1)} %copy-done.26, bf16[384,4096]{1,0:T(8,128)(2,1)} %copy-done.29, bf16[384,4096]{1,0:T(8,128)(2,1)} %copy-done.28, bf16[384,1024]{1,0:T(8,128)(2,1)} %copy-done.27, ...), custom_call_target="tpu_custom_call" | custom-call | tf_op jit(solution)/shard_map/sum_products/pallas_call | solution.py:744
  409.7 5.4 multiply_reduce_fusion.7
  415.7 0.9 copy-done.7
  416.7 1.4 copy-done.61
  418.1 1.9 convolution_convert_fusion.grad_ref
  420.2 0.9 copy-done.20
  421.1 3.5 fusion.44.pos_ref
  424.6 12.2 %attend_back.1 = (bf16[384,1024]{1,0:T(8,128)(2,1)}, bf16[384,1024]{1,0:T(8,128)(2,1)}, bf16[384,1024]{1,0:T(8,128)(2,1)}, bf16[384,1024]{1,0:T(8,128)(2,1)}, f32[2,1024]{1,0:T(2,128)}) custom-call(bf16[384,3072]{1,0:T(8,128)(2,1)} %fusion.10.q_ref.k_ref.v_ref, bf16[384,3072]{1,0:T(8,128)(2,1)} %fusion.10.q_ref.k_ref.v_ref, ...), custom_call_target="tpu_custom_call" | custom-call | tf_op jit(solution)/shard_map/attend_back/pallas_call | solution.py:220
  436.8 1.3 constant_dynamic-update-slice_fusion.2
  438.4 1.2 copy-done.3
  439.6 5.9 multiply_reduce_fusion.8
  446.1 1.5 multiply_convert_fusion.2
  447.7 11.6 %fusion.5.refs_5_ = bf16[384,4096]{1,0:T(8,128)(2,1)S(1)} fusion(f32[384,4096]{1,0:T(8,128)} %get-tuple-element.182, bf16[384,1024]{1,0:T(8,128)(2,1)S(1)} %get-tuple-element.110.refs_7_, bf16[4096,1024]{1,0:T(8,128)(2,1)} %get-tuple-element.52), kind=kOutput, calls=%fused_computation.7 | convolution fusion | flops 3236954112 | bytes 18612224 | tf_op jit(solution)/shard_map/dot_general | solution.py:34
  459.5 3.5 fusion.30
  463.1 1.1 copy-done.12
  464.2 0.8 fusion.26
  465.0 1.3 concatenate.179.refs_10_
  466.3 186.1 %sum_products.3 = (bf16[256,4096]{1,0:T(8,128)(2,1)}, bf16[1024,1024]{1,0:T(8,128)(2,1)}, bf16[256,2048]{1,0:T(8,128)(2,1)}, bf16[256,1024]{1,0:T(8,128)(2,1)}, ...) custom-call(bf16[384,1024]{1,0:T(8,128)(2,1)} %copy-done.19, ...), custom_call_target="tpu_custom_call" | custom-call | tf_op jit(solution)/shard_map/sum_products/pallas_call | solution.py:744
  652.4 4.2 convert_element_type.266
  656.6 2.5 convert_element_type.267
  659.1 2.5 convert_element_type.268
  661.6 2.5 convert_element_type.272
  664.1 2.5 convert_element_type.273
  666.6 1.6 convert_element_type.270
  668.2 1.1 convert_element_type.269
  669.3 1.1 convert_element_type.271
  672.2 1.7 add_add_fusion.6
  (253 shorter events, 19.1 us)
Async XLA Ops:
  2.1 177.8 %copy-start = (bf16[384,1024]{1,0:T(8,128)(2,1)S(1)}, bf16[384,1024]{1,0:T(8,128)(2,1)}, u32[]{:S(2)}) copy-start(bf16[384,1024]{1,0:T(8,128)(2,1)} %param.15) | copy-start | bytes 2359300
  179.9 1.5 copy-start.40
  181.1 10.4 %slice-start.2 = ((s8[8388608]{0:T(1024)(128)(4,1)}), s8[4194304]{0:T(1024)(128)(4,1)S(1)}, s32[]{:S(2)}) async-start(s8[8388608]{0:T(1024)(128)(4,1)} %bitcast.157), calls=%async_computation.2 | async-start | bytes 8388608
  181.1 14.6 %slice-start.4 = ((s8[8388608]{0:T(1024)(128)(4,1)}), s8[4194304]{0:T(1024)(128)(4,1)S(1)}, s32[]{:S(2)}) async-start(s8[8388608]{0:T(1024)(128)(4,1)} %bitcast.159), calls=%async_computation.4 | async-start | bytes 8388608
  181.7 9.9 %copy-start.18 = (bf16[384,1024]{1,0:T(8,128)(2,1)}, bf16[384,1024]{1,0:T(8,128)(2,1)S(1)}, u32[]{:S(2)}) copy-start(bf16[384,1024]{1,0:T(8,128)(2,1)S(1)} %fusion.25.refs_4_) | copy-start | bytes 2359300
  181.7 9.9 %slice-start.3 = ((s8[8388608]{0:T(1024)(128)(4,1)}), s8[4194304]{0:T(1024)(128)(4,1)S(1)}, s32[]{:S(2)}) async-start(s8[8388608]{0:T(1024)(128)(4,1)} %bitcast.157), calls=%async_computation.3 | async-start | bytes 8388608
  181.7 14.1 %slice-start.5 = ((s8[8388608]{0:T(1024)(128)(4,1)}), s8[4194304]{0:T(1024)(128)(4,1)S(1)}, s32[]{:S(2)}) async-start(s8[8388608]{0:T(1024)(128)(4,1)} %bitcast.159), calls=%async_computation.5 | async-start | bytes 8388608
  191.5 3.6 copy-start.21
  195.1 24.0 %copy-start.2 = (f32[384,1024]{1,0:T(8,128)}, f32[384,1024]{1,0:T(8,128)S(1)}, u32[]{:S(2)}) copy-start(f32[384,1024]{1,0:T(8,128)S(1)} %get-tuple-element.184) | copy-start | bytes 4718596
  195.7 3.9 copy-start.19
  195.8 3.9 copy-start.58
  195.8 5.2 copy-start.59
  202.2 6.1 copy-start.53
  219.1 4.2 copy-start.60
  223.3 1.8 copy-start.24
  227.5 4.4 copy-start.54
  227.5 7.7 %copy-start.52 = (s32[192]{0:T(256)S(1)}, s32[192]{0:T(256)}, u32[]{:S(2)}) copy-start(s32[192]{0:T(256)} %copy-done.51) | copy-start | bytes 2308
  236.2 8.7 %slice-start.6 = ((s8[8388608]{0:T(1024)(128)(4,1)}), s8[4194304]{0:T(1024)(128)(4,1)S(1)}, s32[]{:S(2)}) async-start(s8[8388608]{0:T(1024)(128)(4,1)} %bitcast.161), calls=%async_computation.6 | async-start | bytes 8388608
  240.8 1.6 copy-start.62
  241.1 2.1 copy-start.5
  241.1 3.8 slice-start.7
  241.7 2.5 copy-start.25
  244.3 7.1 %slice-start.8 = ((s8[8388608]{0:T(1024)(128)(4,1)}), s8[4194304]{0:T(1024)(128)(4,1)S(1)}, s32[]{:S(2)}) async-start(s8[8388608]{0:T(1024)(128)(4,1)} %bitcast.163), calls=%async_computation.8 | async-start | bytes 8388608
  244.9 6.5 copy-start.26
  244.9 6.4 slice-start.9
  251.4 3.6 copy-start.28
  258.5 11.1 %copy-start.27 = (bf16[384,1024]{1,0:T(8,128)(2,1)}, bf16[384,1024]{1,0:T(8,128)(2,1)S(1)}, u32[]{:S(2)}) copy-start(bf16[384,1024]{1,0:T(8,128)(2,1)S(1)} %multiply_convert_fusion.3.refs_3_) | copy-start | bytes 2359300
  269.6 7.9 %copy-start.29 = (bf16[384,4096]{1,0:T(8,128)(2,1)}, bf16[384,4096]{1,0:T(8,128)(2,1)S(1)}, u32[]{:S(2)}) copy-start(bf16[384,4096]{1,0:T(8,128)(2,1)S(1)} %fusion.2.refs_1_) | copy-start | bytes 9437188
  278.1 2.2 copy-start.63
  279.5 3.0 copy-start.23
  280.2 2.9 copy-start.11
  282.5 1.4 copy-start.8
  282.5 1.9 copy-start.9
  282.5 2.3 copy-start.10
  291.7 117.9 %copy-start.49 = (f32[1024]{0:T(1024)S(1)}, f32[1024]{0:T(1024)}, u32[]{:S(2)}) copy-start(f32[1024]{0:T(1024)} %get-tuple-element.102) | copy-start | bytes 12292
  291.7 118.0 %copy-start.50 = (f32[1024]{0:T(1024)S(1)}, f32[1024]{0:T(1024)}, u32[]{:S(2)}) copy-start(f32[1024]{0:T(1024)} %get-tuple-element.103) | copy-start | bytes 12292
  409.7 5.4 copy-start.6
  416.5 1.6 copy-start.61
  418.1 1.9 copy-start.16
  436.8 1.6 copy-start.36
  438.1 1.5 copy-start.3
  439.6 5.9 copy-start.15
  446.1 13.2 %slice-start = ((s8[8388608]{0:T(1024)(128)(4,1)}), s8[4194304]{0:T(1024)(128)(4,1)S(1)}, s32[]{:S(2)}) async-start(s8[8388608]{0:T(1024)(128)(4,1)} %bitcast.155), calls=%async_computation | async-start | bytes 8388608
  447.7 11.7 %copy-start.17 = (bf16[384,1024]{1,0:T(8,128)(2,1)}, bf16[384,1024]{1,0:T(8,128)(2,1)S(1)}, u32[]{:S(2)}) copy-start(bf16[384,1024]{1,0:T(8,128)(2,1)S(1)} %get-tuple-element.110.refs_7_) | copy-start | bytes 2359300
  447.7 11.7 %copy-start.1 = (bf16[384,1024]{1,0:T(8,128)(2,1)S(1)}, bf16[384,1024]{1,0:T(8,128)(2,1)}, u32[]{:S(2)}) copy-start(bf16[384,1024]{1,0:T(8,128)(2,1)} %param.15) | copy-start | bytes 2359300
  447.7 11.7 %copy-start.41 = (f32[1,2,4,128]{3,1,2,0:T(2,128)S(1)}, f32[1,2,4,128]{3,1,2,0:T(2,128)}, u32[]{:S(2)}) copy-start(f32[1,2,4,128]{3,1,2,0:T(2,128)} %copy-done.40) | copy-start | bytes 12292
  447.7 11.7 %copy-start.43 = (f32[384]{0:T(512)S(1)}, f32[384]{0:T(512)}, u32[]{:S(2)}) copy-start(f32[384]{0:T(512)} %copy-done.42) | copy-start | bytes 4612
  447.7 11.7 %slice-start.1 = ((s8[8388608]{0:T(1024)(128)(4,1)}), s8[4194304]{0:T(1024)(128)(4,1)S(1)}, s32[]{:S(2)}) async-start(s8[8388608]{0:T(1024)(128)(4,1)} %bitcast.155), calls=%async_computation.1 | async-start | bytes 8388608
  459.4 3.6 copy-start.22
  459.4 3.6 copy-start.48
  459.4 4.7 copy-start.45
  463.0 1.9 copy-start.55
  463.0 1.9 copy-start.56
  463.0 1.9 copy-start.57
  652.4 4.3 copy-start.34
  656.6 2.5 copy-start.33
  659.1 2.5 copy-start.32
  661.6 2.5 copy-start.31
  664.1 2.5 copy-start.35
  666.6 1.6 copy-start.39
  666.6 2.7 copy-start.38
  668.2 2.2 copy-start.46
  668.2 4.0 copy-start.13
  668.2 4.0 copy-start.14
  (10 other events, 10.5 us)

commit v3 on v2

--- a/solution.py
+++ b/solution.py
@@ -310,7 +310,7 @@
     return pl.ds(pl.multiple_of(start, 16), count)
 
 
-ORDER = (0, 1, 2, 4, 6, 7, 3, 5)
+ORDER = (4, 0, 1, 2, 6, 7, 3, 5)
 DIRECT = (3, 5)
 
 
@@ -668,7 +668,7 @@
                     spread_open(extra + t)
                 if i == n * (t + 1) + 11:
                     spread_turn(extra + t)
-            at = i - (len(units) - extra)
+            at = i - 1
             if 0 <= at < extra:
                 spread_open(at)
             if 0 <= at - 2 < extra:

time: 678 us -> 674 us (level)
  no operation moved by 1% of the time
where the time goes in v3:
time: 674 us; the launch traced here: 670 us
  Pallas kernels  499 us (74%)
  matrix products  89.8 us (13%)
  other arithmetic  50.6 us (8%)
  local copies, waits for them, and re-layouts  27 us (4%)
    pallas_call x2, Pallas kernels, sum_products(): pl.pallas_call(partial(sums_kernel, n, plan, 0 if small is None else len(...  303 us
    pallas_call x1, Pallas kernels, gather_all(): pl.pallas_call(partial(gather_kernel, n, count), out_shape=[jax.ShapeDtyp...  174 us
    dot_general x8, matrix products, right_product(): lax.dot_general(left_side, right_side, (((1,), (1,)), ((), ())), preferre...  49.6 us
    dot_general x10, matrix products, matmul(): return jnp.dot(left_side, right_side, preferred_element_type=jnp.float32)  40.1 us
    convert_element_type x8, other arithmetic, on_device(): grads = [s.astype(jnp.float32) for s in sums]  17.9 us
    unnamed x164, local copies, waits for them, and re-layouts  14 us

profile of v3, /device:TPU:0, one launch (start us, length us, event | category | flops | bytes accessed | tf_op | source)
XLA Modules:
  0.0 670.4 jit_solution(4743664405848778100)
XLA Ops:
  0.7 1.4 maximum_maximum_fusion.refs_8_
  2.1 173.8 %gather_weights.1 = (bf16[1024,4096]{1,0:T(8,128)(2,1)}, bf16[4096,1024]{1,0:T(8,128)(2,1)}, bf16[1024,4096]{1,0:T(8,128)(2,1)}, bf16[1024,1024]{1,0:T(8,128)(2,...) custom-call(bf16[256,4096]{1,0:T(8,128)(2,1)} %refs_0_.1, ...), custom_call_target="tpu_custom_call" | custom-call | tf_op jit(solution)/shard_map/gather_weights/pallas_call | solution.py:435
  176.0 0.8 copy.43
  178.5 9.9 %multiply_convert_fusion.1 = (bf16[384,4096]{1,0:T(8,128)(2,1)S(1)}, f32[384,4096]{1,0:T(8,128)}) fusion(bf16[384,1024]{1,0:T(8,128)(2,1)S(1)} %fusion.25.refs_4_, bf16[1024,4096]{1,0:T(8,128)(2,1)} %get-tuple-element.51), kind=kOutput, calls=%fused_computation.10 | convolution fusion | flops 3229089792 | bytes 18612224 | tf_op jit(solution)/shard_map/dot_general | solution.py:24
  188.4 3.6 fusion.103
  192.6 3.9 fusion.10.q_ref.k_ref.v_ref
  199.3 0.8 add_convert_fusion.3.allow_ref
  200.6 0.8 multiply_cosine_fusion
  201.6 3.5 fusion.41.pos_ref
  205.1 0.6 copy.32
  205.7 10.2 %attend.1 = (bf16[384,1024]{1,0:T(8,128)(2,1)}, bf16[2,8,192,192]{3,2,1,0:T(8,128)(2,1)}) custom-call(bf16[384,3072]{1,0:T(8,128)(2,1)} %fusion.10.q_ref.k_ref.v_ref, bf16[384,3072]{1,0:T(8,128)(2,1)} %fusion.10.q_ref.k_ref.v_ref, bf16[384,3072]{1,0:T(8,128)(2,1)} %fusion.10.q_ref.k_ref.v_ref, f32[2,1024]{1,0:T(2,128)} %bitcast.105, ...), custom_call_target="tpu_custom_call" | custom-call | tf_op jit(solution)/shard_map/attend/pallas_call | solution.py:197
  215.9 3.0 fusion.104
  220.1 1.8 fusion.107
  222.4 1.9 fusion.92
  224.3 1.9 fusion.93
  226.5 0.7 fusion.67
  228.8 0.8 stack.38
  229.8 0.7 fusion.68
  232.1 0.8 stack.41
  233.0 4.6 fusion.91
  238.6 0.7 copy-done.62
  239.2 0.8 copy-done.5
  240.0 1.1 fusion.105
  241.8 6.4 multiply_convert_fusion
  248.2 3.6 fusion.106
  252.2 0.8 copy-done.30
  252.9 0.6 fusion.28
  253.6 1.5 fusion.90
  255.3 11.1 %fusion.2.refs_1_ = bf16[384,4096]{1,0:T(8,128)(2,1)S(1)} fusion(f32[384,4096]{1,0:T(8,128)} %get-tuple-element.190, bf16[384,1024]{1,0:T(8,128)(2,1)S(1)} %multiply_convert_fusion.3.refs_3_, bf16[4096,1024]{1,0:T(8,128)(2,1)} %get-tuple-element.63), kind=kOutput, calls=%fused_computation.4 | convolution fusion | flops 3236954112 | bytes 18612224 | tf_op jit(solution)/shard_map/dot_general | solution.py:34
  266.4 7.9 %multiply_reduce_fusion.5 = (f32[1024]{0:T(1024)}, f32[384]{0:T(512)S(1)}, f32[384,1024]{1,0:T(8,128)S(1)}) fusion(f32[384,1024]{1,0:T(8,128)S(1)} %get-tuple-element.188, f32[384]{0:T(512)S(1)} %fusion.75, f32[384]{0:T(512)S(1)} %broadcast_multiply_fusion.1, f32[1024]{0:T(1024)S(1)} %bitcast.131, bf16[384,4096]{1,0:T(8,128)(2,1)S(1)} %fusion.2.refs_1_, ...), kind=kOutput, calls=%fused_computation.69 | convolution fusion | flops 3223976448 | bytes 14692864 | tf_op jit(solution)/shard_map/dot_general | solution.py:34
  274.9 1.4 fusion.88
  276.3 0.7 copy-done.63
  277.1 2.3 multiply_reduce_fusion.6
  279.9 0.8 copy-done.8
  281.7 2.7 multiply_reduce_fusion.4
  285.3 1.4 fusion.33
  287.2 1.4 add_convert_fusion.refs_5_
  288.5 119.7 %sum_products.2 = (bf16[32,4096]{1,0:T(8,128)(2,1)}, bf16[128,1024]{1,0:T(8,128)(2,1)}, bf16[32,2048]{1,0:T(8,128)(2,1)}, bf16[32,1024]{1,0:T(8,128)(2,1)}) custom-call(bf16[384,1024]{1,0:T(8,128)(2,1)} %copy-done.26, bf16[384,4096]{1,0:T(8,128)(2,1)} %copy-done.29, bf16[384,4096]{1,0:T(8,128)(2,1)} %copy-done.28, bf16[384,1024]{1,0:T(8,128)(2,1)} %copy-done.27, ...), custom_call_target="tpu_custom_call" | custom-call | tf_op jit(solution)/shard_map/sum_products/pallas_call | solution.py:744
  408.3 5.4 multiply_reduce_fusion.7
  414.3 0.9 copy-done.7
  415.3 1.4 copy-done.61
  416.7 1.9 convolution_convert_fusion.grad_ref
  418.8 0.9 copy-done.20
  419.7 3.5 fusion.44.pos_ref
  423.2 12.2 %attend_back.1 = (bf16[384,1024]{1,0:T(8,128)(2,1)}, bf16[384,1024]{1,0:T(8,128)(2,1)}, bf16[384,1024]{1,0:T(8,128)(2,1)}, bf16[384,1024]{1,0:T(8,128)(2,1)}, f32[2,1024]{1,0:T(2,128)}) custom-call(bf16[384,3072]{1,0:T(8,128)(2,1)} %fusion.10.q_ref.k_ref.v_ref, bf16[384,3072]{1,0:T(8,128)(2,1)} %fusion.10.q_ref.k_ref.v_ref, ...), custom_call_target="tpu_custom_call" | custom-call | tf_op jit(solution)/shard_map/attend_back/pallas_call | solution.py:220
  435.4 1.3 constant_dynamic-update-slice_fusion.2
  437.0 1.2 copy-done.3
  438.2 5.9 multiply_reduce_fusion.8
  444.7 1.5 multiply_convert_fusion.2
  446.3 11.6 %fusion.5.refs_5_ = bf16[384,4096]{1,0:T(8,128)(2,1)S(1)} fusion(f32[384,4096]{1,0:T(8,128)} %get-tuple-element.182, bf16[384,1024]{1,0:T(8,128)(2,1)S(1)} %get-tuple-element.110.refs_7_, bf16[4096,1024]{1,0:T(8,128)(2,1)} %get-tuple-element.52), kind=kOutput, calls=%fused_computation.7 | convolution fusion | flops 3236954112 | bytes 18612224 | tf_op jit(solution)/shard_map/dot_general | solution.py:34
  458.0 3.5 fusion.30
  461.7 1.1 copy-done.12
  462.8 0.8 fusion.26
  463.6 1.3 concatenate.179.refs_10_
  464.9 183.5 %sum_products.3 = (bf16[256,4096]{1,0:T(8,128)(2,1)}, bf16[1024,1024]{1,0:T(8,128)(2,1)}, bf16[256,2048]{1,0:T(8,128)(2,1)}, bf16[256,1024]{1,0:T(8,128)(2,1)}, ...) custom-call(bf16[384,1024]{1,0:T(8,128)(2,1)} %copy-done.19, ...), custom_call_target="tpu_custom_call" | custom-call | tf_op jit(solution)/shard_map/sum_products/pallas_call | solution.py:744
  648.4 4.2 convert_element_type.266
  652.7 2.5 convert_element_type.267
  655.2 2.5 convert_element_type.268
  657.7 2.5 convert_element_type.272
  660.2 2.5 convert_element_type.273
  662.7 1.6 convert_element_type.270
  664.2 1.1 convert_element_type.269
  665.3 1.1 convert_element_type.271
  668.2 1.7 add_add_fusion.6
  (253 shorter events, 19.1 us)
Async XLA Ops:
  2.1 174.7 %copy-start = (bf16[384,1024]{1,0:T(8,128)(2,1)S(1)}, bf16[384,1024]{1,0:T(8,128)(2,1)}, u32[]{:S(2)}) copy-start(bf16[384,1024]{1,0:T(8,128)(2,1)} %param.15) | copy-start | bytes 2359300
  176.8 1.5 copy-start.40
  177.9 10.4 %slice-start.2 = ((s8[8388608]{0:T(1024)(128)(4,1)}), s8[4194304]{0:T(1024)(128)(4,1)S(1)}, s32[]{:S(2)}) async-start(s8[8388608]{0:T(1024)(128)(4,1)} %bitcast.157), calls=%async_computation.2 | async-start | bytes 8388608
  177.9 14.6 %slice-start.4 = ((s8[8388608]{0:T(1024)(128)(4,1)}), s8[4194304]{0:T(1024)(128)(4,1)S(1)}, s32[]{:S(2)}) async-start(s8[8388608]{0:T(1024)(128)(4,1)} %bitcast.159), calls=%async_computation.4 | async-start | bytes 8388608
  178.5 9.9 %copy-start.18 = (bf16[384,1024]{1,0:T(8,128)(2,1)}, bf16[384,1024]{1,0:T(8,128)(2,1)S(1)}, u32[]{:S(2)}) copy-start(bf16[384,1024]{1,0:T(8,128)(2,1)S(1)} %fusion.25.refs_4_) | copy-start | bytes 2359300
  178.5 9.9 %slice-start.3 = ((s8[8388608]{0:T(1024)(128)(4,1)}), s8[4194304]{0:T(1024)(128)(4,1)S(1)}, s32[]{:S(2)}) async-start(s8[8388608]{0:T(1024)(128)(4,1)} %bitcast.157), calls=%async_computation.3 | async-start | bytes 8388608
  178.5 14.1 %slice-start.5 = ((s8[8388608]{0:T(1024)(128)(4,1)}), s8[4194304]{0:T(1024)(128)(4,1)S(1)}, s32[]{:S(2)}) async-start(s8[8388608]{0:T(1024)(128)(4,1)} %bitcast.159), calls=%async_computation.5 | async-start | bytes 8388608
  188.4 3.6 copy-start.21
  191.9 24.0 %copy-start.2 = (f32[384,1024]{1,0:T(8,128)}, f32[384,1024]{1,0:T(8,128)S(1)}, u32[]{:S(2)}) copy-start(f32[384,1024]{1,0:T(8,128)S(1)} %get-tuple-element.184) | copy-start | bytes 4718596
  192.5 3.9 copy-start.19
  192.6 3.9 copy-start.58
  192.6 5.2 copy-start.59
  199.0 6.1 copy-start.53
  215.9 4.2 copy-start.60
  220.1 1.8 copy-start.24
  224.3 4.4 copy-start.54
  224.3 7.7 %copy-start.52 = (s32[192]{0:T(256)S(1)}, s32[192]{0:T(256)}, u32[]{:S(2)}) copy-start(s32[192]{0:T(256)} %copy-done.51) | copy-start | bytes 2308
  233.0 8.7 %slice-start.6 = ((s8[8388608]{0:T(1024)(128)(4,1)}), s8[4194304]{0:T(1024)(128)(4,1)S(1)}, s32[]{:S(2)}) async-start(s8[8388608]{0:T(1024)(128)(4,1)} %bitcast.161), calls=%async_computation.6 | async-start | bytes 8388608
  237.6 1.6 copy-start.62
  237.9 2.1 copy-start.5
  238.0 3.8 slice-start.7
  238.6 2.5 copy-start.25
  241.1 7.1 %slice-start.8 = ((s8[8388608]{0:T(1024)(128)(4,1)}), s8[4194304]{0:T(1024)(128)(4,1)S(1)}, s32[]{:S(2)}) async-start(s8[8388608]{0:T(1024)(128)(4,1)} %bitcast.163), calls=%async_computation.8 | async-start | bytes 8388608
  241.7 6.5 copy-start.26
  241.8 6.4 slice-start.9
  248.2 3.6 copy-start.28
  255.3 11.1 %copy-start.27 = (bf16[384,1024]{1,0:T(8,128)(2,1)}, bf16[384,1024]{1,0:T(8,128)(2,1)S(1)}, u32[]{:S(2)}) copy-start(bf16[384,1024]{1,0:T(8,128)(2,1)S(1)} %multiply_convert_fusion.3.refs_3_) | copy-start | bytes 2359300
  266.4 7.9 %copy-start.29 = (bf16[384,4096]{1,0:T(8,128)(2,1)}, bf16[384,4096]{1,0:T(8,128)(2,1)S(1)}, u32[]{:S(2)}) copy-start(bf16[384,4096]{1,0:T(8,128)(2,1)S(1)} %fusion.2.refs_1_) | copy-start | bytes 9437188
  274.9 2.2 copy-start.63
  276.3 3.0 copy-start.23
  277.1 2.9 copy-start.11
  279.3 1.4 copy-start.8
  279.4 1.9 copy-start.9
  279.4 2.3 copy-start.10
  288.5 119.7 %copy-start.49 = (f32[1024]{0:T(1024)S(1)}, f32[1024]{0:T(1024)}, u32[]{:S(2)}) copy-start(f32[1024]{0:T(1024)} %get-tuple-element.102) | copy-start | bytes 12292
  288.5 119.7 %copy-start.50 = (f32[1024]{0:T(1024)S(1)}, f32[1024]{0:T(1024)}, u32[]{:S(2)}) copy-start(f32[1024]{0:T(1024)} %get-tuple-element.103) | copy-start | bytes 12292
  408.3 5.4 copy-start.6
  415.1 1.6 copy-start.61
  416.7 1.9 copy-start.16
  435.4 1.6 copy-start.36
  436.7 1.5 copy-start.3
  438.2 5.9 copy-start.15
  444.7 13.2 %slice-start = ((s8[8388608]{0:T(1024)(128)(4,1)}), s8[4194304]{0:T(1024)(128)(4,1)S(1)}, s32[]{:S(2)}) async-start(s8[8388608]{0:T(1024)(128)(4,1)} %bitcast.155), calls=%async_computation | async-start | bytes 8388608
  446.3 11.7 %copy-start.17 = (bf16[384,1024]{1,0:T(8,128)(2,1)}, bf16[384,1024]{1,0:T(8,128)(2,1)S(1)}, u32[]{:S(2)}) copy-start(bf16[384,1024]{1,0:T(8,128)(2,1)S(1)} %get-tuple-element.110.refs_7_) | copy-start | bytes 2359300
  446.3 11.7 %copy-start.1 = (bf16[384,1024]{1,0:T(8,128)(2,1)S(1)}, bf16[384,1024]{1,0:T(8,128)(2,1)}, u32[]{:S(2)}) copy-start(bf16[384,1024]{1,0:T(8,128)(2,1)} %param.15) | copy-start | bytes 2359300
  446.3 11.7 %copy-start.41 = (f32[1,2,4,128]{3,1,2,0:T(2,128)S(1)}, f32[1,2,4,128]{3,1,2,0:T(2,128)}, u32[]{:S(2)}) copy-start(f32[1,2,4,128]{3,1,2,0:T(2,128)} %copy-done.40) | copy-start | bytes 12292
  446.3 11.7 %copy-start.43 = (f32[384]{0:T(512)S(1)}, f32[384]{0:T(512)}, u32[]{:S(2)}) copy-start(f32[384]{0:T(512)} %copy-done.42) | copy-start | bytes 4612
  446.3 11.7 %slice-start.1 = ((s8[8388608]{0:T(1024)(128)(4,1)}), s8[4194304]{0:T(1024)(128)(4,1)S(1)}, s32[]{:S(2)}) async-start(s8[8388608]{0:T(1024)(128)(4,1)} %bitcast.155), calls=%async_computation.1 | async-start | bytes 8388608
  458.0 3.6 copy-start.22
  458.0 3.6 copy-start.48
  458.0 4.7 copy-start.45
  461.6 1.9 copy-start.55
  461.6 1.9 copy-start.56
  461.6 1.9 copy-start.57
  648.4 4.3 copy-start.34
  652.7 2.5 copy-start.33
  655.2 2.5 copy-start.32
  657.7 2.5 copy-start.31
  660.2 2.5 copy-start.35
  662.7 1.6 copy-start.39
  662.7 2.7 copy-start.38
  664.2 2.2 copy-start.46
  664.2 4.0 copy-start.13
  664.2 4.0 copy-start.14
  (10 other events, 10.5 us)
